TPU v7x, 32 devices: a whole 2x2x4 slice. The times are simulated.
32 devices in a mesh: groups: 2 (over x), row: 8 (over z, y), col: 2 (over core).
Axes of the slice: x: 2, y: 2, z: 4, core: 2. Of those that a mesh axis runs over, the one named last changes fastest.
Arguments:
- tokens_in: bfloat16 [16, 256, 768], P('groups', 'row'), parts along dimension 0, may hold values from -6 to 6
- cond_single: bfloat16 [512, 768], P(('groups', 'row')), parts along dimension 0, may hold values from -6 to 6
- token_mask: int32 [512], P(('groups', 'row')), parts along dimension 0, may hold values 0 or 1
- pair_cond: bfloat16 [512, 256, 128], P(('groups', 'row'), 'col'), parts along dimension 0, may hold values from -1000 to 1000
- w_pair: bfloat16 [128, 16], replicated, may hold values from -0.5 to 0.5
- w_scale: bfloat16 [768, 768], replicated, may hold values from -0.21875 to 0.21875
- w_shift: bfloat16 [768, 768], replicated, may hold values from -0.21875 to 0.21875
- w_outgate: bfloat16 [768, 768], replicated, may hold values from -0.21875 to 0.21875
- w_query: bfloat16 [768, 768], P(None, 'col'), may hold values from -0.21875 to 0.21875
- w_key: bfloat16 [768, 768], P(None, 'col'), may hold values from -0.21875 to 0.21875
- w_value: bfloat16 [768, 768], P(None, 'col'), may hold values from -0.21875 to 0.21875
- w_gate: bfloat16 [768, 768], P(None, 'col'), may hold values from -0.21875 to 0.21875
- w_out: bfloat16 [768, 768], P('col'), may hold values from -0.21875 to 0.21875
- atom_cond: bfloat16 [4096, 128], P(('groups', 'row', 'col')), parts along dimension 0, may hold values from -6 to 6
- atom_token: int32 [4096], P(('groups', 'row', 'col')), parts along dimension 0, may hold values from 0 to 255, as said below
- window_start: int32 [128], P(('groups', 'row', 'col')), parts along dimension 0, may hold values from 0 to 1920, as said below
- atom_mask: int32 [4096], P(('groups', 'row', 'col')), parts along dimension 0, may hold values 0 or 1
- atom_pair: bfloat16 [128, 16, 32, 128], P(('groups', 'row', 'col')), parts along dimension 0, may hold values from -1000 to 1000
- w_token_atom: bfloat16 [768, 128], replicated, may hold values from -0.21875 to 0.21875
- w_ascale: bfloat16 [128, 128], replicated, may hold values from -0.5 to 0.5
- w_ashift: bfloat16 [128, 128], replicated, may hold values from -0.5 to 0.5
- w_aquery: bfloat16 [128, 128], replicated, may hold values from -0.5 to 0.5
- w_akey: bfloat16 [128, 128], replicated, may hold values from -0.5 to 0.5
- w_avalue: bfloat16 [128, 128], replicated, may hold values from -0.5 to 0.5
- w_agate: bfloat16 [128, 128], replicated, may hold values from -0.5 to 0.5
- w_aout: bfloat16 [128, 128], replicated, may hold values from -0.5 to 0.5
- w_apair: bfloat16 [16, 4], replicated, may hold values from -1.5 to 1.5
- w_update: bfloat16 [3, 128], replicated, may hold values from -0.5 to 0.5
Outputs:
- tokens_out: bfloat16 [16, 256, 768], P('groups', 'row'), parts along dimension 0
- atom_update: float32 [16, 3, 2048], P('groups', None, ('row', 'col')), parts along dimension 0
There are 2 independent parts, one for each index of `groups`. A program takes and returns all parts, laid end to end along the dimension named above; an argument that names none is the same for every part. Nothing has to cross between parts.
Inputs may be any that keep to these rules, and one draw needn't show every extreme that they name: atom_token[l] differs from l // 8 by at most 16. window_start[k] differs from k * 32 + 32 // 2 - 128 // 2 by at most 16, unless it is clipped to the range.
All inputs are finite; a program needn't handle non-finite values. No bound on the sum of `token_mask` or of `atom_mask` on one device may be relied on, other than what follows from the above.
Results may differ from a plain program's by a relative error of at most 0.0075.
Values may be sent and summed in bfloat16 or wider, within the bound.
No kernel may reach another device: no remote copies, remote signals or barrier semaphores. Data moves between devices by JAX's collectives and lax.ppermute only.
A program may use at most 128 MiB of HBM per device.

v0:
```python
import jax
import jax.numpy as jnp
from jax import lax
from jax.sharding import PartitionSpec as P

HEAD = 48
AHEADS = 4
AHEAD = 32
WQ = 32
WK = 128


def extended_2(cells, sides, width):
    for axis, dim in sides:
        count = lax.axis_size(axis)
        ends = count - 1
        head = lax.slice_in_dim(cells, 0, width, axis=dim)
        tail = lax.slice_in_dim(cells, cells.shape[dim] - width, cells.shape[dim], axis=dim)
        cells = jnp.concatenate(
            [
                lax.ppermute(tail, axis, [(i, (i + 1) % count) for i in range(ends)]),
                cells,
                lax.ppermute(head, axis, [((i + 1) % count, i) for i in range(ends)]),
            ],
            axis=dim,
        )
    return cells


def layer_norm(inputs):
    inputs = inputs.astype(jnp.float32)
    centred = inputs - jnp.mean(inputs, axis=-1, keepdims=True)
    variance = jnp.mean(centred * centred, axis=-1, keepdims=True)
    return centred * lax.rsqrt(variance + 1e-05)


def project_rows(sample_rows, w_token_atom):
    token_norm = layer_norm(sample_rows).astype(jnp.bfloat16)
    return jnp.einsum(
        "std,de->ste", token_norm, w_token_atom, preferred_element_type=jnp.float32
    ).astype(jnp.bfloat16)


def shards(
    tokens_in,
    cond_single,
    token_mask,
    pair_cond,
    w_pair,
    w_scale,
    w_shift,
    w_outgate,
    w_query,
    w_key,
    w_value,
    w_gate,
    w_out,
    atom_cond,
    atom_token,
    window_start,
    atom_mask,
    atom_pair,
    w_token_atom,
    w_ascale,
    w_ashift,
    w_aquery,
    w_akey,
    w_avalue,
    w_agate,
    w_aout,
    w_apair,
    w_update,
):
    samples, tok_rows, feature_width = tokens_in.shape
    local_heads = w_query.shape[1] // HEAD
    inv_root = HEAD ** (-0.5)
    cond_norm = layer_norm(cond_single).astype(jnp.bfloat16)
    ada_scale = jax.nn.sigmoid(jnp.dot(cond_norm, w_scale, preferred_element_type=jnp.float32))
    ada_shift = jnp.dot(cond_norm, w_shift, preferred_element_type=jnp.float32)
    out_gate = jax.nn.sigmoid(jnp.dot(cond_norm, w_outgate, preferred_element_type=jnp.float32))
    local_bias = jnp.einsum("ijc,ch->hij", pair_cond, w_pair, preferred_element_type=jnp.float32)
    pair_bias = lax.all_to_all(local_bias, "col", split_axis=0, concat_axis=2, tiled=True)
    mixed_rows = (ada_scale[None] * layer_norm(tokens_in) + ada_shift[None]).astype(jnp.bfloat16)
    queries = (
        jnp.einsum("sqd,de->sqe", mixed_rows, w_query, preferred_element_type=jnp.float32)
        * inv_root
    ).astype(jnp.bfloat16)
    queries = queries.reshape(samples, tok_rows, local_heads, HEAD)
    key_rows = jnp.einsum(
        "sqd,de->sqe", mixed_rows, w_key, preferred_element_type=jnp.float32
    ).astype(jnp.bfloat16)
    value_rows = jnp.einsum(
        "sqd,de->sqe", mixed_rows, w_value, preferred_element_type=jnp.float32
    ).astype(jnp.bfloat16)
    head_gate = jax.nn.sigmoid(
        jnp.einsum("sqd,de->sqe", mixed_rows, w_gate, preferred_element_type=jnp.float32)
    )
    stacked = jnp.stack([key_rows, value_rows])
    mask_row = token_mask.astype(jnp.bfloat16).reshape(1, 1, tok_rows)
    row_max = jnp.full((samples, local_heads, tok_rows), -1e30, jnp.float32)
    kv_piece = lax.all_gather(stacked, "row", axis=2, tiled=True)
    mask_piece = lax.all_gather(mask_row, "row", axis=2, tiled=True)
    key_count = kv_piece.shape[2]
    piece_keys = kv_piece[0].reshape(samples, key_count, local_heads, HEAD)
    piece_values = kv_piece[1].reshape(samples, key_count, local_heads, HEAD)
    mask_shift = ((mask_piece.astype(jnp.float32) - 1.0) * 10000.0).reshape(1, 1, 1, key_count)
    scores = (
        jnp.einsum("sqhd,skhd->shqk", queries, piece_keys, preferred_element_type=jnp.float32)
        + pair_bias[None]
        + mask_shift
    )
    new_max = jnp.maximum(row_max, jnp.max(scores, axis=-1))
    weights = jnp.exp(scores - new_max[..., None])
    totals = jnp.sum(weights, axis=-1)
    summed = jnp.einsum(
        "shqk,skhd->shqd",
        weights.astype(jnp.bfloat16),
        piece_values,
        preferred_element_type=jnp.float32,
    )
    row_max, totals, summed = (new_max, totals, summed)
    attended = jnp.transpose(summed / totals[..., None], (0, 2, 1, 3)).reshape(
        samples, tok_rows, local_heads * HEAD
    )
    gated = (head_gate * attended).astype(jnp.bfloat16)
    partial_value = jnp.einsum("sqe,ed->sqd", gated, w_out, preferred_element_type=jnp.float32)
    update = lax.psum(partial_value.astype(jnp.bfloat16), "col").astype(jnp.float32)
    tokens_out = (tokens_in.astype(jnp.float32) + out_gate[None] * update).astype(jnp.bfloat16)
    projected = project_rows(tokens_out, w_token_atom)
    lookup = extended_2(projected, (("row", 1),), tok_rows // 2)
    local_token = atom_token - (lax.axis_index("row") * tok_rows - tok_rows // 2)
    atom_rows = atom_cond.shape[0]
    local_windows = atom_rows // WQ
    cond_anorm = layer_norm(atom_cond).astype(jnp.bfloat16)
    atom_scale = jax.nn.sigmoid(jnp.dot(cond_anorm, w_ascale, preferred_element_type=jnp.float32))
    atom_shift = jnp.dot(cond_anorm, w_ashift, preferred_element_type=jnp.float32)
    atom_state = atom_cond.astype(jnp.float32)[None] + jnp.take(lookup, local_token, axis=1).astype(
        jnp.float32
    )
    atom_mixed = (atom_scale[None] * layer_norm(atom_state) + atom_shift[None]).astype(jnp.bfloat16)
    atom_root = AHEAD ** (-0.5)
    atom_queries = (
        jnp.einsum("sad,de->sae", atom_mixed, w_aquery, preferred_element_type=jnp.float32)
        * atom_root
    ).astype(jnp.bfloat16)
    atom_queries = atom_queries.reshape(samples, local_windows, WQ, AHEADS, AHEAD)
    atom_gate = jax.nn.sigmoid(
        jnp.einsum("sad,de->sae", atom_mixed, w_agate, preferred_element_type=jnp.float32)
    )
    atom_keys = jnp.einsum(
        "sad,de->sae", atom_mixed, w_akey, preferred_element_type=jnp.float32
    ).astype(jnp.bfloat16)
    atom_values = jnp.einsum(
        "sad,de->sae", atom_mixed, w_avalue, preferred_element_type=jnp.float32
    ).astype(jnp.bfloat16)
    extended = extended_2(jnp.stack([atom_keys, atom_values]), ((("row", "col"), 2),), WK // 2)
    wide_keys = extended[0]
    wide_values = extended[1]
    window_offset = window_start - (lax.axis_index(("row", "col")) * atom_rows - WK // 2)
    key_index = window_offset[:, None] + jnp.arange(WK, dtype=jnp.int32)[None, :]
    window_keys = jnp.take(wide_keys, key_index, axis=1).reshape(
        samples, local_windows, WK, AHEADS, AHEAD
    )
    window_values = jnp.take(wide_values, key_index, axis=1).reshape(
        samples, local_windows, WK, AHEADS, AHEAD
    )
    atom_bias = jnp.einsum("wcqk,ch->whqk", atom_pair, w_apair, preferred_element_type=jnp.float32)
    atom_scores = (
        jnp.einsum(
            "swqhd,swkhd->swhqk", atom_queries, window_keys, preferred_element_type=jnp.float32
        )
        + atom_bias[None]
    )
    atom_max = jnp.max(atom_scores, axis=-1, keepdims=True)
    atom_weights = jnp.exp(atom_scores - atom_max)
    atom_totals = jnp.sum(atom_weights, axis=-1, keepdims=True)
    atom_attended = jnp.einsum(
        "swhqk,swkhd->swqhd",
        atom_weights.astype(jnp.bfloat16),
        window_values,
        preferred_element_type=jnp.float32,
    )
    atom_attended = atom_attended / jnp.transpose(atom_totals, (0, 1, 3, 2, 4))
    atom_gated = (atom_gate * atom_attended.reshape(samples, atom_rows, AHEADS * AHEAD)).astype(
        jnp.bfloat16
    )
    atom_final = atom_state + jnp.einsum(
        "sad,de->sae", atom_gated, w_aout, preferred_element_type=jnp.float32
    )
    final_norm = layer_norm(atom_final).astype(jnp.bfloat16)
    atom_update = jnp.einsum(
        "cd,sad->sca", w_update, final_norm, preferred_element_type=jnp.float32
    )
    atom_update = atom_update * atom_mask.astype(jnp.float32)[None, None, :]
    return (tokens_out, atom_update)


def solution(mesh):
    return jax.shard_map(
        shards,
        mesh=mesh,
        in_specs=(
            P("groups", "row", None),
            P(("groups", "row"), None),
            P(("groups", "row")),
            P(("groups", "row"), "col", None),
            P(),
            P(),
            P(),
            P(),
            P(None, "col"),
            P(None, "col"),
            P(None, "col"),
            P(None, "col"),
            P("col", None),
            P(("groups", "row", "col"), None),
            P(("groups", "row", "col")),
            P(("groups", "row", "col")),
            P(("groups", "row", "col")),
            P(("groups", "row", "col"), None, None, None),
            P(),
            P(),
            P(),
            P(),
            P(),
            P(),
            P(),
            P(),
            P(),
            P(),
        ),
        out_specs=(P("groups", "row", None), P("groups", None, ("row", "col"))),
        check_vma=False,
    )
```

profile of v0, /device:TPU:1, one launch (start us, length us, event | category | flops | bytes accessed | tf_op | source)
XLA Modules:
  0.0 169.0 jit_solution(7626165011451416089)
XLA Ops:
  7.2 1.1 convert_reduce_fusion.2
  8.3 1.0 fusion.78
  9.3 1.2 fusion.27
  10.5 1.7 %fusion.97 = f32[32,768]{1,0:T(8,128)S(1)} fusion(bf16[768,768]{1,0:T(8,128)(2,1)} %param.36, bf16[32,768]{1,0:T(8,128)(2,1)} %param.31, f32[32]{0:T(128)S(1)} %add_rsqrt_fusion.5, f32[32]{0:T(128)S(1)} %broadcast_multiply_fusion.5), kind=kOutput, calls=%fused_computation.164 | convolution fusion | flops 37847040 | bytes 1327360 | tf_op jit(solution)/shard_map/dot_general | solution.py:79
  12.7 0.5 fusion.20
  13.2 0.5 fusion.21
  13.7 0.8 pad_maximum_fusion.1
  14.5 0.4 fusion.86
  14.9 0.8 copy.68
  15.7 3.6 %all-to-all-start = ((f32[16,32,128]{2,1,0:T(8,128)}), f32[16,32,128]{2,1,0:T(8,128)S(1)}, u32[]{:S(2)}, u32[]{:S(2)}) async-start(f32[16,32,128]{2,1,0:T(8,128)} %copy.68), calls=%async_computation | async-start | bytes 524288 | tf_op jit(solution)/shard_map/all_to_all | solution.py:82
  19.4 0.5 fusion.16
  19.8 1.2 reshape.125
  21.1 1.3 dynamic-slice
  23.4 19.7 %all-reduce = bf16[256]{0:T(256)(128)(2,1)S(1)} all-reduce(bf16[256]{0:T(256)(128)(2,1)S(1)} %dynamic-update-slice), channel_id=2, replica_groups=mesh['groups'=2,'row'=8,'col'=2] {'row'}, use_global_device_ids=true, to_apply=%add | all-reduce | flops 256 | bytes 1024
  43.4 0.7 broadcast_subtract_fusion
  44.1 0.5 add_multiply_fusion
  44.6 0.6 compare_and_fusion
  45.3 1.6 fusion.30
  46.9 0.9 fusion.96
  47.8 1.0 convolution_bitcast_fusion.1
  48.8 26.3 %all-gather.3.cloned.1.call-done = bf16[2,8,256,384]{3,2,1,0:T(8,128)(2,1)} async-done(((bf16[2,8,32,384]{3,2,1,0:T(8,128)(2,1)}), bf16[2,8,256,384]{3,2,1,0:T(8,128)(2,1)}) %all-gather.3.cloned.1.call-update) | async-done | bytes 3145744 | tf_op jit(solution)/shard_map/all_gather | solution.py:101
  75.1 3.4 %fusion.112 = (bf16[1,8,256,384]{3,2,1,0:T(8,128)(2,1)S(1)}, bf16[1,8,256,384]{3,2,1,0:T(8,128)(2,1)}) fusion(bf16[2,8,256,384]{3,2,1,0:T(8,128)(2,1)} %all-gather.3.cloned.1.call-done), kind=kLoop, calls=%fused_computation.165 | loop fusion | bytes 6291456 | tf_op jit(solution)/shard_map/slice | solution.py:104
  78.6 1.7 copy.66
  80.2 2.0 %fusion = (f32[8,8,32]{2,1,0:T(8,128)S(1)}, f32[8,8,32,256]{3,2,1,0:T(8,128)S(1)}) fusion(f32[256]{0:T(256)} %add_multiply_fusion, f32[8,32,256]{2,1,0:T(8,128)S(1)} %bitcast.138, bf16[8,256,8,48]{1,3,2,0:T(8,128)(2,1)} %bitcast.134, bf16[8,32,8,48]{3,2,1,0:T(8,128)(2,1)} %reshape.125), kind=kOutput, calls=%fused_computation.8 | convolution fusion | flops 51902464 | bytes 4137984 | tf_op jit(solution)/shard_map/sqhd,skhd->shqk/dot_general | solution.py:108
  82.3 0.6 broadcast_maximum_fusion
  82.9 2.6 %copy.70 = bf16[1,8,256,384]{2,3,1,0:T(8,128)(2,1)} copy(bf16[1,8,256,384]{3,2,1,0:T(8,128)(2,1)} %get-tuple-element.14) | data formatting | bytes 3145728 | tf_op jit(solution)/shard_map/slice | solution.py:105
  85.5 1.6 fusion.3
  87.1 0.8 fusion.5
  88.0 0.6 copy.71
  89.0 2.8 %convolution_convert_fusion = bf16[8,32,768]{2,1,0:T(8,128)(2,1)} fusion(f32[8,32,384]{2,1,0:T(8,128)S(1)} %reshape.127, bf16[384,768]{1,0:T(8,128)(2,1)} %param.42, bf16[768,384]{1,0:T(8,128)(2,1)} %param.41, bf16[8,32,768]{2,1,0:T(8,128)(2,1)S(1)} %copy-done.2, f32[32,768]{1,0:T(8,128)S(1)} %copy-done.19, f32[8,32]{1,0:T(8,128)S(1)} %copy-done.28, ...), kind=kOutput, calls=%fused_computation.15 | convolution fusion | flops 303857664 | bytes 2557952 | tf_op jit(solution)/shard_map/sqe,ed->sqd/dot_general | solution.py:126
  91.9 0.6 fusion.91
  92.5 1.7 fusion.25
  94.2 17.0 %all-reduce.3.cloned.1.call-done = bf16[8,32,768]{2,1,0:T(8,128)(2,1)} async-done(((bf16[8,32,768]{2,1,0:T(8,128)(2,1)}), bf16[8,32,768]{2,1,0:T(8,128)(2,1)}) %all-reduce.3.cloned.1.call-update) | async-done | bytes 393232 | tf_op jit(solution)/shard_map/psum | solution.py:127
  111.2 1.2 convert_reduce_fusion.1
  112.7 0.4 copy-done.6
  113.2 0.3 convolution_convert_fusion.5
  113.6 3.4 %collective-permute-start = (bf16[8,16,128]{2,1,0:T(8,128)(2,1)S(1)}, bf16[8,16,128]{2,1,0:T(8,128)(2,1)S(1)}, u32[]{:S(2)}, u32[]{:S(2)}) collective-permute-start(bf16[8,16,128]{2,1,0:T(8,128)(2,1)S(1)} %get-tuple-element.19), channel_id=1, source_target_pairs={{0,2},{2,4},{4,6},{6,8},{8,10},{10,12},{12,14},{1,3},{3,5},{5,7},{... | collective-permute-start | bytes 98312 | tf_op jit(solution)/shard_map/ppermute | solution.py:21
  117.0 1.3 collective-permute-start.1
  118.5 3.1 %collective-permute-done.1 = bf16[8,16,128]{2,1,0:T(8,128)(2,1)S(1)} collective-permute-done((bf16[8,16,128]{2,1,0:T(8,128)(2,1)S(1)}, bf16[8,16,128]{2,1,0:T(8,128)(2,1)S(1)}, u32[]{:S(2)}, u32[]{:S(2)}) %collective-permute-start.1) | collective-permute-done | bytes 32800 | tf_op jit(solution)/shard_map/ppermute | solution.py:23
  121.7 0.7 gather_fusion
  123.0 0.3 fusion.19
  123.3 0.3 fusion.18
  123.7 0.8 fusion.70
  124.4 5.6 %collective-permute-start.2 = (bf16[2,8,64,128]{3,2,1,0:T(8,128)(2,1)}, bf16[2,8,64,128]{3,2,1,0:T(8,128)(2,1)}, u32[]{:S(2)}, u32[]{:S(2)}) collective-permute-start(bf16[2,8,64,128]{3,2,1,0:T(8,128)(2,1)} %get-tuple-element.17), channel_id=1, source_target_pairs={{0,1},{1,2},{2,3},{3,4},{4,5},{5,6},{6,7},{7,8},{8,9},{9,10},{10,1... | collective-permute-start | bytes 786440 | tf_op jit(solution)/shard_map/ppermute | solution.py:21
  130.0 2.1 %collective-permute-start.3 = (bf16[2,8,64,128]{3,2,1,0:T(8,128)(2,1)S(1)}, bf16[2,8,64,128]{3,2,1,0:T(8,128)(2,1)}, u32[]{:S(2)}, u32[]{:S(2)}) collective-permute-start(bf16[2,8,64,128]{3,2,1,0:T(8,128)(2,1)S(1)} %get-tuple-element.18), channel_id=1, source_target_pairs={{1,0},{2,1},{3,2},{4,3},{5,4},{6,5},{7,6},{8,7},{9,8},{10,9},{11,1... | collective-permute-start | bytes 786440 | tf_op jit(solution)/shard_map/ppermute | solution.py:23
  132.2 0.5 convert_element_type.113
  132.7 0.3 fusion.11
  133.0 0.4 reshape.129
  133.6 4.2 %collective-permute-done.3 = bf16[2,8,64,128]{3,2,1,0:T(8,128)(2,1)} collective-permute-done((bf16[2,8,64,128]{3,2,1,0:T(8,128)(2,1)S(1)}, bf16[2,8,64,128]{3,2,1,0:T(8,128)(2,1)}, u32[]{:S(2)}, u32[]{:S(2)}) %collective-permute-start.3) | collective-permute-done | bytes 262176 | tf_op jit(solution)/shard_map/ppermute | solution.py:23
  137.8 1.1 pad_maximum_fusion
  139.0 0.3 copy.80
  139.3 0.3 copy.83
  139.7 2.4 %gather_fusion.1 = bf16[512,8,128]{2,1,0:T(8,128)(2,1)} fusion(bf16[8,256,128]{2,0,1:T(8,128)(2,1)S(1)} %copy.80, s32[1024]{0:T(1024)S(1)} %pad_clamp_fusion), kind=kCustom, calls=%fused_computation.clone | custom fusion | bytes 2099200 | tf_op jit(solution)/shard_map/jit(_take)/gather | solution.py:164
  142.1 2.4 %gather_fusion.2 = bf16[512,8,128]{2,1,0:T(8,128)(2,1)} fusion(bf16[8,256,128]{2,0,1:T(8,128)(2,1)S(1)} %copy.83, s32[1024]{0:T(1024)S(1)} %pad_clamp_fusion), kind=kCustom, calls=%fused_computation.1.clone | custom fusion | bytes 2099200 | tf_op jit(solution)/shard_map/jit(_take)/gather | solution.py:161
  144.5 2.9 %select_bitcast_fusion = (bf16[8,4,128,128]{3,0,2,1:T(8,128)(2,1)}, bf16[8,4,128,128]{3,0,2,1:T(8,128)(2,1)}) fusion(bf16[4,128,8,128]{3,2,1,0:T(8,128)(2,1)} %bitcast.136, pred[4,128]{1,0:T(4,128)(4,1)S(1)} %copy-done.34, bf16[4,128,8,128]{3,2,1,0:T(8,128)(2,1)} %bitcast.135), kind=kLoop, calls=%fused_computation.63 | loop fusion | flops 1048576 | bytes 4194816 | tf_op jit(solution)/shard_map/jit(_take)/select_n | solution.py:161
  147.4 1.7 %copy.84 = bf16[8,4,128,128]{2,3,1,0:T(8,128)(2,1)S(1)} copy(bf16[8,4,128,128]{3,0,2,1:T(8,128)(2,1)} %get-tuple-element.21) | data formatting | bytes 2097152 | tf_op jit(solution)/shard_map/jit(_take)/select_n | solution.py:161
  149.1 2.4 %copy.81 = bf16[8,4,128,128]{2,3,1,0:T(8,128)(2,1)} copy(bf16[8,4,128,128]{3,0,2,1:T(8,128)(2,1)} %get-tuple-element.22) | data formatting | bytes 2097152 | tf_op jit(solution)/shard_map/jit(_take)/select_n | solution.py:164
  151.6 0.8 add_reduce_fusion
  152.4 1.4 fusion.1
  153.8 2.0 %bitcast_divide_fusion = f32[8,4,32,4,32]{2,4,3,1,0:T(8,128)} fusion(bf16[8,4,128,4,32]{2,4,3,1,0:T(8,128)(2,1)S(1)} %bitcast.142, f32[8,4,4,32,128]{4,3,2,1,0:T(8,128)S(1)} %get-tuple-element.26, f32[8,4,32,4]{2,3,1,0:T(4,128)S(1)} %bitcast.144, f32[8,4,4,32]{3,2,1,0:T(4,128)S(1)} %get-tuple-element.25, f32[4,4,32,128]{3,2,1,0:T(8,128)S(1)} %copy.87), kind=kOutput, calls=%fused_computation.3 | convolution fusion | flops 35258368 | bytes 3964928 | tf_op jit(solution)/shard_map/swhqk,swkhd->swqhd/dot_general | solution.py:177
  155.8 2.1 %copy.88 = f32[8,4,32,4,32]{4,3,2,1,0:T(4,128)S(1)} copy(f32[8,4,32,4,32]{2,4,3,1,0:T(8,128)} %bitcast_divide_fusion) | data formatting | bytes 1048576 | tf_op jit(solution)/shard_map/div | solution.py:183
  157.9 1.7 reshape.131
  159.6 1.7 %fusion.114 = (f32[8,128]{1,0:T(8,128)S(1)}, f32[8,128,128]{1,2,0:T(8,128)S(1)}) fusion(bf16[128,128]{1,0:T(8,128)(2,1)} %param.55, f32[8,128,128]{2,1,0:T(8,128)} %reshape.131, bf16[128,128]{1,0:T(8,128)(2,1)} %param.54, f32[128,128]{0,1:T(8,128)} %copy-done.11, f32[128,128]{0,1:T(8,128)} %fusion.96, f32[8,128]{1,0:T(8,128)S(1)} %copy-done.30, ...), kind=kOutput, calls=%fused_computation.167 | convolution fusion | flops 69467136 | bytes 1585280 | tf_op jit(solution)/shard_map/sad,de->sae/dot_general | solution.py:187
  161.6 0.6 copy.91
  (139 shorter events, 3.2 us)
Async XLA Ops:
  7.2 2.1 %copy-start = (bf16[768,768]{1,0:T(8,128)(2,1)S(1)}, bf16[768,768]{1,0:T(8,128)(2,1)}, u32[]{:S(2)}) copy-start(bf16[768,768]{1,0:T(8,128)(2,1)} %param.35) | copy-start | bytes 3538948
  7.2 5.1 %copy-start.1 = (bf16[8,32,768]{2,1,0:T(8,128)(2,1)S(1)}, bf16[8,32,768]{2,1,0:T(8,128)(2,1)}, u32[]{:S(2)}) copy-start(bf16[8,32,768]{2,1,0:T(8,128)(2,1)} %param.30) | copy-start | bytes 1179652
  7.2 5.5 %copy-start.39 = (bf16[768,384]{1,0:T(8,128)(2,1)S(1)}, bf16[768,384]{1,0:T(8,128)(2,1)}, u32[]{:S(2)}) copy-start(bf16[768,384]{1,0:T(8,128)(2,1)} %param.39) | copy-start | bytes 1769476
  7.2 67.9 %all-gather.3.cloned.1.call-start = ((), (), s32[]{:S(2)}) async-start(), calls=%async_computation.1 | async-start | bytes 3538944 | tf_op jit(solution)/shard_map/all_gather | solution.py:101
  10.5 8.8 %copy-start.16 = (f32[32,768]{1,0:T(8,128)}, f32[32,768]{1,0:T(8,128)S(1)}, u32[]{:S(2)}) copy-start(f32[32,768]{1,0:T(8,128)S(1)} %fusion.27) | copy-start | bytes 294916
  10.5 2.7 %copy-start.40 = (bf16[768,384]{1,0:T(8,128)(2,1)S(1)}, bf16[768,384]{1,0:T(8,128)(2,1)}, u32[]{:S(2)}) copy-start(bf16[768,384]{1,0:T(8,128)(2,1)} %param.40) | copy-start | bytes 1769476
  12.3 7.1 %copy-start.18 = (f32[32,768]{1,0:T(8,128)}, f32[32,768]{1,0:T(8,128)S(1)}, u32[]{:S(2)}) copy-start(f32[32,768]{1,0:T(8,128)S(1)} %fusion.97) | copy-start | bytes 294916
  12.7 6.7 %copy-start.27 = (f32[8,32]{1,0:T(8,128)}, f32[8,32]{1,0:T(8,128)S(1)}, u32[]{:S(2)}) copy-start(f32[8,32]{1,0:T(8,128)S(1)} %add_rsqrt_fusion.3) | copy-start | bytes 3076
  12.7 1.8 %copy-start.8 = (bf16[32,128,128]{2,1,0:T(8,128)(2,1)S(1)}, bf16[32,128,128]{2,1,0:T(8,128)(2,1)}, u32[]{:S(2)}) copy-start(bf16[32,128,128]{2,1,0:T(8,128)(2,1)} %param.33) | copy-start | bytes 3145732
  12.7 1.8 %copy-start.25 = (bf16[128,16]{0,1:T(8,128)(2,1)S(1)}, bf16[128,16]{0,1:T(8,128)(2,1)}, u32[]{:S(2)}) copy-start(bf16[128,16]{0,1:T(8,128)(2,1)} %param.34) | copy-start | bytes 12292
  13.7 5.7 %copy-start.41 = (bf16[768,384]{1,0:T(8,128)(2,1)S(1)}, bf16[768,384]{1,0:T(8,128)(2,1)}, u32[]{:S(2)}) copy-start(bf16[768,384]{1,0:T(8,128)(2,1)} %param.38) | copy-start | bytes 1769476
  14.9 6.2 %copy-start.46 = (s32[32]{0:T(128)S(1)}, s32[32]{0:T(128)}, u32[]{:S(2)}) copy-start(s32[32]{0:T(128)} %param.32) | copy-start | bytes 388
  14.9 28.2 %copy-start.13 = (bf16[128,128]{1,0:T(8,128)(2,1)S(1)}, bf16[128,128]{1,0:T(8,128)(2,1)}, u32[]{:S(2)}) copy-start(bf16[128,128]{1,0:T(8,128)(2,1)} %param.43) | copy-start | bytes 98308
  14.9 29.8 %copy-start.38 = (s32[128]{0:T(128)S(1)}, s32[128]{0:T(128)}, u32[]{:S(2)}) copy-start(s32[128]{0:T(128)} %param.44) | copy-start | bytes 1540
  15.7 31.2 %copy-start.23 = (bf16[128,128]{1,0:T(8,128)(2,1)S(1)}, bf16[128,128]{1,0:T(8,128)(2,1)}, u32[]{:S(2)}) copy-start(bf16[128,128]{1,0:T(8,128)(2,1)} %param.50) | copy-start | bytes 98308
  15.7 32.1 %copy-start.12 = (bf16[4,16,32,128]{3,2,1,0:T(8,128)(2,1)S(1)}, bf16[4,16,32,128]{3,2,1,0:T(8,128)(2,1)}, u32[]{:S(2)}) copy-start(bf16[4,16,32,128]{3,2,1,0:T(8,128)(2,1)} %param.47) | copy-start | bytes 1572868
  15.7 32.1 %copy-start.32 = (bf16[16,4]{0,1:T(4,128)(2,1)S(1)}, bf16[16,4]{0,1:T(4,128)(2,1)}, u32[]{:S(2)}) copy-start(bf16[16,4]{0,1:T(4,128)(2,1)} %param.56) | copy-start | bytes 388
  15.7 5.4 %all-to-all-start = ((f32[16,32,128]{2,1,0:T(8,128)}), f32[16,32,128]{2,1,0:T(8,128)S(1)}, u32[]{:S(2)}, u32[]{:S(2)}) async-start(f32[16,32,128]{2,1,0:T(8,128)} %copy.68), calls=%async_computation | async-start | bytes 524288 | tf_op jit(solution)/shard_map/all_to_all | solution.py:82
  19.3 91.9 %all-reduce.3.cloned.1.call-start = ((), (), s32[]{:S(2)}) async-start(), calls=%async_computation.2 | async-start | bytes 786432 | tf_op jit(solution)/shard_map/psum | solution.py:127
  44.1 4.7 %copy-start.36 = (s32[4]{0:T(128)}, s32[4]{0:T(128)S(1)}, u32[]{:S(2)}) copy-start(s32[4]{0:T(128)S(1)} %broadcast_subtract_fusion) | copy-start | bytes 52
  85.5 1.6 copy-start.5
  85.5 1.6 copy-start.15
  85.5 1.6 copy-start.26
  87.9 1.0 copy-start.2
  87.9 1.0 copy-start.17
  88.0 1.0 copy-start.19
  88.0 1.0 copy-start.28
  89.0 2.8 %copy-start.37 = (s32[4]{0:T(128)S(1)}, s32[4]{0:T(128)}, u32[]{:S(2)}) copy-start(s32[4]{0:T(128)} %copy-done.36) | copy-start | bytes 52
  89.0 3.5 %copy-start.7 = (bf16[32,768]{1,0:T(8,128)(2,1)S(1)}, bf16[32,768]{1,0:T(8,128)(2,1)}, u32[]{:S(2)}) copy-start(bf16[32,768]{1,0:T(8,128)(2,1)} %param.31) | copy-start | bytes 147460
  91.8 21.4 %copy-start.42 = (bf16[768,128]{1,0:T(8,128)(2,1)S(1)}, bf16[768,128]{1,0:T(8,128)(2,1)}, u32[]{:S(2)}) copy-start(bf16[768,128]{1,0:T(8,128)(2,1)} %param.48) | copy-start | bytes 589828
  91.9 26.4 %copy-start.31 = (s32[128]{0:T(128)S(1)}, s32[128]{0:T(128)}, u32[]{:S(2)}) copy-start(s32[128]{0:T(128)} %get-tuple-element.10) | copy-start | bytes 1540
  91.9 26.4 %copy-start.14 = (bf16[128,128]{1,0:T(8,128)(2,1)S(1)}, bf16[128,128]{1,0:T(8,128)(2,1)}, u32[]{:S(2)}) copy-start(bf16[128,128]{1,0:T(8,128)(2,1)} %param.43) | copy-start | bytes 98308
  92.5 25.9 %copy-start.22 = (f32[128,128]{1,0:T(8,128)S(1)}, f32[128,128]{1,0:T(8,128)}, u32[]{:S(2)}) copy-start(f32[128,128]{1,0:T(8,128)} %fusion.30) | copy-start | bytes 196612
  94.2 28.5 %copy-start.24 = (pred[128]{0:T(512)(128)(4,1)S(1)}, pred[128]{0:T(512)(128)(4,1)}, u32[]{:S(2)}) copy-start(pred[128]{0:T(512)(128)(4,1)} %get-tuple-element.9) | copy-start | bytes 388
  112.4 0.7 copy-start.6
  112.5 10.5 %copy-start.20 = (f32[128,128]{0,1:T(8,128)S(1)}, f32[128,128]{0,1:T(8,128)}, u32[]{:S(2)}) copy-start(f32[128,128]{0,1:T(8,128)} %fusion.96) | copy-start | bytes 196612
  112.5 10.5 %copy-start.43 = (bf16[128,128]{1,0:T(8,128)(2,1)S(1)}, bf16[128,128]{1,0:T(8,128)(2,1)}, u32[]{:S(2)}) copy-start(bf16[128,128]{1,0:T(8,128)(2,1)} %param.53) | copy-start | bytes 98308
  113.2 10.1 %copy-start.44 = (bf16[128,128]{1,0:T(8,128)(2,1)S(1)}, bf16[128,128]{1,0:T(8,128)(2,1)}, u32[]{:S(2)}) copy-start(bf16[128,128]{1,0:T(8,128)(2,1)} %param.52) | copy-start | bytes 98308
  113.6 5.0 %collective-permute-start = (bf16[8,16,128]{2,1,0:T(8,128)(2,1)S(1)}, bf16[8,16,128]{2,1,0:T(8,128)(2,1)S(1)}, u32[]{:S(2)}, u32[]{:S(2)}) collective-permute-start(bf16[8,16,128]{2,1,0:T(8,128)(2,1)S(1)} %get-tuple-element.19), channel_id=1, source_target_pairs={{0,2},{2,4},{4,6},{6,8},{8,10},{10,12},{12,14},{1,3},{3,5},{5,7},{... | collective-permute-start | bytes 98312 | tf_op jit(solution)/shard_map/ppermute | solution.py:21
  117.0 4.7 %collective-permute-start.1 = (bf16[8,16,128]{2,1,0:T(8,128)(2,1)S(1)}, bf16[8,16,128]{2,1,0:T(8,128)(2,1)S(1)}, u32[]{:S(2)}, u32[]{:S(2)}) collective-permute-start(bf16[8,16,128]{2,1,0:T(8,128)(2,1)S(1)} %get-tuple-element.20), channel_id=1, source_target_pairs={{2,0},{4,2},{6,4},{8,6},{10,8},{12,10},{14,12},{3,1},{5,3},{7,5},{... | collective-permute-start | bytes 98312 | tf_op jit(solution)/shard_map/ppermute | solution.py:23
  118.4 14.3 %copy-start.11 = (f32[128,128]{0,1:T(8,128)}, f32[128,128]{0,1:T(8,128)S(1)}, u32[]{:S(2)}) copy-start(f32[128,128]{0,1:T(8,128)S(1)} %copy.72) | copy-start | bytes 196612
  118.5 14.2 %copy-start.21 = (f32[128,128]{0,1:T(8,128)}, f32[128,128]{0,1:T(8,128)S(1)}, u32[]{:S(2)}) copy-start(f32[128,128]{0,1:T(8,128)S(1)} %copy.75) | copy-start | bytes 196612
  122.4 9.7 %copy-start.10 = (f32[4,4,32,128]{3,1,2,0:T(4,128)S(1)}, f32[4,4,32,128]{3,1,2,0:T(4,128)}, u32[]{:S(2)}) copy-start(f32[4,4,32,128]{3,1,2,0:T(4,128)} %convolution_bitcast_fusion.1) | copy-start | bytes 786436
  122.7 10.0 %copy-start.3 = (bf16[128,8,128]{0,2,1:T(8,128)(2,1)}, bf16[128,8,128]{0,2,1:T(8,128)(2,1)S(1)}, u32[]{:S(2)}) copy-start(bf16[128,8,128]{0,2,1:T(8,128)(2,1)S(1)} %copy.74) | copy-start | bytes 786436
  122.8 9.4 %copy-start.47 = (s32[128]{0:T(128)S(1)}, s32[128]{0:T(128)}, u32[]{:S(2)}) copy-start(s32[128]{0:T(128)} %param.46) | copy-start | bytes 1540
  122.8 9.9 %copy-start.45 = (bf16[128,128]{1,0:T(8,128)(2,1)S(1)}, bf16[128,128]{1,0:T(8,128)(2,1)}, u32[]{:S(2)}) copy-start(bf16[128,128]{1,0:T(8,128)(2,1)} %param.51) | copy-start | bytes 98308
  123.0 9.7 %copy-start.29 = (f32[8,128]{1,0:T(8,128)}, f32[8,128]{1,0:T(8,128)S(1)}, u32[]{:S(2)}) copy-start(f32[8,128]{1,0:T(8,128)S(1)} %add_rsqrt_fusion.1) | copy-start | bytes 12292
  124.4 9.2 %collective-permute-start.2 = (bf16[2,8,64,128]{3,2,1,0:T(8,128)(2,1)}, bf16[2,8,64,128]{3,2,1,0:T(8,128)(2,1)}, u32[]{:S(2)}, u32[]{:S(2)}) collective-permute-start(bf16[2,8,64,128]{3,2,1,0:T(8,128)(2,1)} %get-tuple-element.17), channel_id=1, source_target_pairs={{0,1},{1,2},{2,3},{3,4},{4,5},{5,6},{6,7},{7,8},{8,9},{9,10},{10,1... | collective-permute-start | bytes 786440 | tf_op jit(solution)/shard_map/ppermute | solution.py:21
  130.0 7.8 %collective-permute-start.3 = (bf16[2,8,64,128]{3,2,1,0:T(8,128)(2,1)S(1)}, bf16[2,8,64,128]{3,2,1,0:T(8,128)(2,1)}, u32[]{:S(2)}, u32[]{:S(2)}) collective-permute-start(bf16[2,8,64,128]{3,2,1,0:T(8,128)(2,1)S(1)} %get-tuple-element.18), channel_id=1, source_target_pairs={{1,0},{2,1},{3,2},{4,3},{5,4},{6,5},{7,6},{8,7},{9,8},{10,9},{11,1... | collective-permute-start | bytes 786440 | tf_op jit(solution)/shard_map/ppermute | solution.py:23
  139.7 4.8 %copy-start.34 = (pred[4,128]{1,0:T(4,128)(4,1)S(1)}, pred[4,128]{1,0:T(4,128)(4,1)}, u32[]{:S(2)}) copy-start(pred[4,128]{1,0:T(4,128)(4,1)} %fusion.91) | copy-start | bytes 1540
  152.4 1.4 copy-start.9
  157.9 1.7 %copy-start.4 = (bf16[128,8,128]{0,2,1:T(8,128)(2,1)S(1)}, bf16[128,8,128]{0,2,1:T(8,128)(2,1)}, u32[]{:S(2)}) copy-start(bf16[128,8,128]{0,2,1:T(8,128)(2,1)} %copy-done.3) | copy-start | bytes 786436
  157.9 1.7 %copy-start.30 = (f32[8,128]{1,0:T(8,128)S(1)}, f32[8,128]{1,0:T(8,128)}, u32[]{:S(2)}) copy-start(f32[8,128]{1,0:T(8,128)} %copy-done.29) | copy-start | bytes 12292
  159.6 1.8 %copy-start.33 = (bf16[3,128]{1,0:T(4,128)(2,1)S(1)}, bf16[3,128]{1,0:T(4,128)(2,1)}, u32[]{:S(2)}) copy-start(bf16[3,128]{1,0:T(4,128)(2,1)} %param.57) | copy-start | bytes 2308
  159.6 1.8 %copy-start.35 = (f32[128]{0:T(128)S(1)}, f32[128]{0:T(128)}, u32[]{:S(2)}) copy-start(f32[128]{0:T(128)} %convert_element_type.113) | copy-start | bytes 1540
Sparse Core Ops, SparseCore 0:
  14.6 60.4 all-gather.2
  92.0 19.2 all-reduce.2
where the time goes:
time: 170 us; the launch traced here: 169 us
  waiting for transfers between devices  50.8 us (30%)
  local copies, waits for them, and re-layouts  28.7 us (17%)
  matrix products  21.5 us (13%)
  blocking collectives  19.7 us (12%)
  other arithmetic  16.6 us (10%)
  starting transfers between devices  16 us (9%)
  between operations  15.7 us (9%)
    all_gather x1, waiting for transfers between devices, shards(): kv_piece = lax.all_gather(stacked, 'row', axis=2, tiled=True)  26.3 us
    unnamed x1, blocking collectives  19.7 us
    psum x1, waiting for transfers between devices, shards(): lax.psum(partial_value.astype(jnp.bfloat16), 'col').astype(jnp.float32)  17 us
    ppermute x2, starting transfers between devices, extended_2(): lax.ppermute(tail, axis, [(i, (i + 1) % count) for i in range(ends)])  8.97 us
    ppermute x2, waiting for transfers between devices, extended_2(): lax.ppermute(head, axis, [((i + 1) % count, i) for i in range(ends)])  7.27 us
    slice x2, local copies, waits for them, and re-layouts, shards(): piece_keys = kv_piece[0].reshape(samples, key_count, local_heads, HEAD)  5.09 us
    all_to_all x1, starting transfers between devices, shards(): lax.all_to_all(local_bias, 'col', split_axis=0, concat_axis=2, tiled=True)  3.59 us
  transfers between devices with their start and end apart: 7, of which 5 were waited for; matrix products, arithmetic and copies ran while one was open for 8% of the time, Pallas kernels for 0%

commit v1 on v0

v1 whole, which is shorter than its diff:
```python
import functools

import jax
import jax.numpy as jnp
from jax import lax
from jax.experimental import pallas as pl
from jax.experimental.pallas import tpu as pltpu
from jax.sharding import PartitionSpec as P

HEAD = 48
AHEADS = 4
AHEAD = 32
WQ = 32
WK = 128
HALO = WK // 2
SPAN = 2 * WK
PER_TOKEN = 8
F32 = jnp.float32
BF16 = jnp.bfloat16
NT = (((1,), (1,)), ((), ()))


def layer_norm(inputs):
    inputs = inputs.astype(F32)
    centred = inputs - jnp.mean(inputs, axis=-1, keepdims=True)
    variance = jnp.mean(centred * centred, axis=-1, keepdims=True)
    return centred * lax.rsqrt(variance + 1e-05)


def dot(a, b):
    return jnp.dot(a, b, preferred_element_type=F32)


def whole(array):
    zeros = (0,) * array.ndim
    return pl.BlockSpec(array.shape, lambda *_: zeros)


def of(shape, dtype):
    return jax.ShapeDtypeStruct(shape, dtype)


def mix_kernel(col_ref, tok_ref, cond_ref, scale_ref, shift_ref, valid_ref, out_ref):
    samples, rows, _ = tok_ref.shape
    cond_norm = layer_norm(cond_ref[...]).astype(BF16)
    scale = jax.nn.sigmoid(dot(cond_norm, scale_ref[...]))
    shift = dot(cond_norm, shift_ref[...])
    for s in range(samples):
        mixed = scale * layer_norm(tok_ref[s]) + shift
        out_ref[s * rows : (s + 1) * rows, :] = mixed.astype(BF16)
    out_ref[samples * rows :, :] = valid_ref[...]


def mix(col, tokens_in, cond, w_scale, w_shift, valid, local_samples):
    _, rows, width = tokens_in.shape
    total = local_samples * rows + valid.shape[0]
    return pl.pallas_call(
        mix_kernel,
        grid_spec=pltpu.PrefetchScalarGridSpec(
            num_scalar_prefetch=1,
            grid=(1,),
            in_specs=[
                pl.BlockSpec((local_samples, rows, width), lambda i, c: (c[0], 0, 0)),
                whole(cond),
                whole(w_scale),
                whole(w_shift),
                whole(valid),
            ],
            out_specs=pl.BlockSpec((total, width), lambda i, c: (0, 0)),
        ),
        out_shape=of((total, width), BF16),
        name="mix",
    )(col, tokens_in, cond, w_scale, w_shift, valid)


def kv_kernel(count, aliased, place_ref, *refs):
    blocks, refs = refs[:count], refs[count:]
    weights, refs = refs[:4], refs[4:]
    key_ref, value_ref = refs[2:] if aliased else refs
    samples, rows, _ = key_ref.shape
    block = blocks[0][...]
    if count == 2:
        first = pl.program_id(0) == 0
        block = jnp.where(first, block, blocks[1][...])
    half = weights[0].shape[1]
    for index, weight in enumerate(weights):
        out = dot(block, weight[...]).astype(BF16).reshape(samples, rows, half)
        target = key_ref if index < 2 else value_ref
        start = (index % 2) * half
        target[:, :, start : start + half] = out


def project_kv(place, base, blocks, weights, held, samples, rows, keys):
    count = len(blocks)
    width = blocks[0].shape[1]
    aliased = held is not None
    held = held or ()
    out_spec = pl.BlockSpec((samples, rows, width), lambda i, p: (0, p[base + i], 0))
    return pl.pallas_call(
        functools.partial(kv_kernel, count, aliased),
        grid_spec=pltpu.PrefetchScalarGridSpec(
            num_scalar_prefetch=1,
            grid=(count,),
            in_specs=[pl.BlockSpec((samples * rows, width), lambda i, p: (0, 0))] * count
            + [whole(w) for w in weights]
            + [pl.BlockSpec(memory_space=pl.ANY)] * len(held),
            out_specs=[out_spec, out_spec],
        ),
        out_shape=[of((samples, keys, width), BF16)] * 2,
        input_output_aliases={1 + count + 4 + i: i for i in range(len(held))},
        name="project_kv",
    )(place, *blocks, *weights, *held)


def query_kernel(root, block_ref, ql_ref, qr_ref, gl_ref, gr_ref, cond_ref, og_ref, q_ref, g_ref, o_ref):
    block = block_ref[...]
    half = ql_ref.shape[1]
    q_ref[:, :half] = (dot(block, ql_ref[...]) * root).astype(BF16)
    q_ref[:, half:] = (dot(block, qr_ref[...]) * root).astype(BF16)
    g_ref[:, :half] = jax.nn.sigmoid(dot(block, gl_ref[...]))
    g_ref[:, half:] = jax.nn.sigmoid(dot(block, gr_ref[...]))
    cond_norm = layer_norm(cond_ref[...]).astype(BF16)
    o_ref[...] = jax.nn.sigmoid(dot(cond_norm, og_ref[...]))


def project_q(block, weights, cond, w_outgate, count):
    width = block.shape[1]
    rows = cond.shape[0]
    return pl.pallas_call(
        functools.partial(query_kernel, HEAD ** (-0.5)),
        grid=(1,),
        in_specs=[pl.BlockSpec((count, width), lambda i: (0, 0))]
        + [whole(w) for w in weights]
        + [whole(cond), whole(w_outgate)],
        out_specs=[pl.BlockSpec((count, width), lambda i: (0, 0))] * 2
        + [pl.BlockSpec((rows, width), lambda i: (0, 0))],
        out_shape=[of((count, width), BF16), of((count, width), F32), of((rows, width), F32)],
        name="project_q",
    )(block, *weights, cond, w_outgate)


def bias_kernel(pair_ref, w_ref, out_ref):
    rows, keys, channels = pair_ref.shape
    for i in range(rows):
        out_ref[:, i, :] = lax.dot_general(
            w_ref[...], pair_ref[i], NT, preferred_element_type=F32
        )


def pair_bias_of(pair_cond, w_pair):
    rows, keys, _ = pair_cond.shape
    heads = w_pair.shape[1]
    return pl.pallas_call(
        bias_kernel, out_shape=of((heads, rows, keys), F32), name="pair_bias"
    )(pair_cond, w_pair.T)


def head_lanes(shape, start, head, size):
    lane = lax.broadcasted_iota(jnp.int32, shape, 1) + start
    return (lane >= head * size) & (lane < (head + 1) * size)


def attend_kernel(
    blocks, valid_width, col_ref, q_ref, k_ref, v_ref, bl_ref, br_ref, g_ref, o_ref, tok_ref, wol_ref,
    wor_ref, wta_ref, *refs,
):
    valid_refs, (out_ref, proj_ref, gated_ref) = refs[:blocks], refs[blocks:]
    s = pl.program_id(0)
    col = col_ref[0]
    rows, width = q_ref.shape
    heads = bl_ref.shape[0]
    half = heads // 2
    query = q_ref[...].astype(F32)
    spread = jnp.concatenate(
        [
            jnp.where(head_lanes((rows, width), 0, h, HEAD), query, 0.0).astype(BF16)
            for h in range(heads)
        ],
        axis=0,
    )
    keys = k_ref[0]
    scores = lax.dot_general(spread, keys, NT, preferred_element_type=F32)
    valid = valid_refs[0][...].astype(F32)
    for ref in valid_refs[1:]:
        valid = valid + ref[...].astype(F32)
    count = keys.shape[0]
    shift = jnp.concatenate(
        [valid[i : i + 1, :valid_width] for i in range(count // valid_width)], axis=1
    )
    shift = (shift - 1.0) * 10000.0
    near = pl.multiple_of(col * half, half)
    far = pl.multiple_of((1 - col) * half, half)
    bias = jnp.concatenate(
        [
            jnp.concatenate([ref[pl.ds(near, half)], ref[pl.ds(far, half)]], axis=0).reshape(
                heads * rows, ref.shape[2]
            )
            for ref in (bl_ref, br_ref)
        ],
        axis=1,
    )
    scores = scores + bias + shift
    weights = jnp.exp(scores - jnp.max(scores, axis=-1, keepdims=True))
    totals = jnp.sum(weights, axis=-1, keepdims=True)
    weights = weights.astype(BF16)
    start = pl.multiple_of(s * rows, rows)
    for lane in range(0, width, 128):
        low, high = lane // HEAD, (lane + 127) // HEAD + 1
        part = dot(weights[low * rows : high * rows], v_ref[0, :, lane : lane + 128])
        attended = jnp.zeros((rows, 128), F32)
        for h in range(low, high):
            mine = part[(h - low) * rows : (h - low + 1) * rows] / totals[h * rows : (h + 1) * rows]
            attended = attended + jnp.where(head_lanes((rows, 128), lane, h, HEAD), mine, 0.0)
        gate = g_ref[pl.ds(start, rows), lane : lane + 128]
        gated_ref[pl.ds(start, rows), lane : lane + 128] = (gate * attended).astype(BF16)

    @pl.when(s == pl.num_programs(0) - 1)
    def _():
        gated = gated_ref[...]
        middle = wol_ref.shape[0]
        update = dot(gated[:, :middle], wol_ref[...]) + dot(gated[:, middle:], wor_ref[...])
        samples = tok_ref.shape[0]
        for n in range(samples):
            tokens = tok_ref[n].astype(F32) + o_ref[...] * update[n * rows : (n + 1) * rows]
            tokens = tokens.astype(BF16)
            out_ref[n] = tokens
            proj_ref[n] = dot(layer_norm(tokens).astype(BF16), wta_ref[...]).astype(BF16)


def attend(col, query, keys, values, near, far, gate, out_gate, tokens_in, outs, w_token_atom, blocks, valid_width):
    samples, count, width = keys.shape
    rows = query.shape[0] // samples
    atoms = w_token_atom.shape[1]
    per_sample = pl.BlockSpec((1, count, width), lambda s, c: (s, 0, 0))
    valid_row = samples * rows // 8
    return pl.pallas_call(
        functools.partial(attend_kernel, len(blocks), valid_width),
        grid_spec=pltpu.PrefetchScalarGridSpec(
            num_scalar_prefetch=1,
            grid=(samples,),
            in_specs=[
                pl.BlockSpec((rows, width), lambda s, c: (s, 0)),
                per_sample,
                per_sample,
                whole(near),
                whole(far),
                whole(gate),
                whole(out_gate),
                pl.BlockSpec((samples, rows, width), lambda s, c: (c[0], 0, 0)),
                whole(outs[0]),
                whole(outs[1]),
                whole(w_token_atom),
            ]
            + [pl.BlockSpec((8, width), lambda s, c: (valid_row, 0))] * len(blocks),
            out_specs=[
                pl.BlockSpec((samples, rows, width), lambda s, c: (0, 0, 0)),
                pl.BlockSpec((samples, rows, atoms), lambda s, c: (0, 0, 0)),
            ],
            scratch_shapes=[pltpu.VMEM((samples * rows, width), BF16)],
        ),
        out_shape=[of((samples, rows, width), BF16), of((samples, rows, atoms), BF16)],
        name="attend",
    )(col, query, keys, values, near, far, gate, out_gate, tokens_in, *outs, w_token_atom, *blocks)


def atom_bias_kernel(w_ref, pair_ref, out_ref):
    windows, channels, rows, keys = pair_ref.shape
    heads = w_ref.shape[1]

    def window(k, carry):
        pair = [pair_ref[k, c].astype(F32) for c in range(channels)]
        for h in range(heads):
            total = pair[0] * w_ref[0, h]
            for c in range(1, channels):
                total = total + pair[c] * w_ref[c, h]
            out_ref[k, h * rows : (h + 1) * rows, :] = total
        return carry

    lax.fori_loop(0, windows, window, 0)


def atom_bias_of(atom_pair, w_apair):
    windows, _, rows, keys = atom_pair.shape
    heads = w_apair.shape[1]
    return pl.pallas_call(
        atom_bias_kernel,
        in_specs=[pl.BlockSpec(memory_space=pltpu.SMEM), pl.BlockSpec(memory_space=pltpu.VMEM)],
        out_shape=of((windows, heads * rows, keys), F32),
        name="atom_bias",
    )(w_apair.astype(F32), atom_pair)


def atom_cond_kernel(cond_ref, scale_ref, shift_ref, out_scale_ref, out_shift_ref):
    cond_norm = layer_norm(cond_ref[...]).astype(BF16)
    out_scale_ref[...] = jax.nn.sigmoid(dot(cond_norm, scale_ref[...]))
    out_shift_ref[...] = dot(cond_norm, shift_ref[...])


def atom_cond_of(cond, w_ascale, w_ashift):
    return pl.pallas_call(
        atom_cond_kernel, out_shape=[of(cond.shape, F32)] * 2, name="atom_cond"
    )(cond, w_ascale, w_ashift)


def atom_kernel(
    col_ref, left_ref, own_ref, right_ref, pick_ref, win_ref, cond_ref, scale_ref, shift_ref, bias_ref,
    live_ref, wq_ref, wk_ref, wv_ref, wg_ref, wo_ref, wu_ref, keep_ref, send_ref,
):
    samples = own_ref.shape[0]
    extent, width = cond_ref.shape
    windows = win_ref.shape[0]
    atoms = windows * WQ
    pick = pick_ref[...]
    cond = cond_ref[...].astype(F32)
    scale, shift = scale_ref[...], shift_ref[...]
    root = AHEAD ** (-0.5)
    mine = col_ref[0] == 0
    for s in range(samples):
        lookup = jnp.concatenate([left_ref[s], own_ref[s], right_ref[s]], axis=0)
        state = cond + dot(pick, lookup)
        mixed = (scale * layer_norm(state) + shift).astype(BF16)
        inner = mixed[HALO : HALO + atoms]
        query = dot(inner, wq_ref[...]) * root
        gate = jax.nn.sigmoid(dot(inner, wg_ref[...]))
        keys = dot(mixed, wk_ref[...]).astype(BF16)
        values = dot(mixed, wv_ref[...]).astype(BF16)
        pieces = []
        for k in range(windows):
            base = min(max(k * WQ - WQ, 0), extent - SPAN)
            window = win_ref[k]
            window_keys = dot(window, keys[base : base + SPAN]).astype(BF16)
            window_values = dot(window, values[base : base + SPAN]).astype(BF16)
            own = query[k * WQ : (k + 1) * WQ]
            spread = jnp.concatenate(
                [
                    jnp.where(head_lanes((WQ, width), 0, h, AHEAD), own, 0.0).astype(BF16)
                    for h in range(AHEADS)
                ],
                axis=0,
            )
            scores = lax.dot_general(spread, window_keys, NT, preferred_element_type=F32)
            scores = scores + bias_ref[k]
            weights = jnp.exp(scores - jnp.max(scores, axis=-1, keepdims=True))
            totals = jnp.sum(weights, axis=-1, keepdims=True)
            part = dot(weights.astype(BF16), window_values) / totals
            attended = jnp.zeros((WQ, width), F32)
            for h in range(AHEADS):
                attended = attended + jnp.where(
                    head_lanes((WQ, width), 0, h, AHEAD), part[h * WQ : (h + 1) * WQ], 0.0
                )
            pieces.append(attended)
        gated = (gate * jnp.concatenate(pieces, axis=0)).astype(BF16)
        final = state[HALO : HALO + atoms] + dot(gated, wo_ref[...])
        final = layer_norm(final).astype(BF16)
        update = lax.dot_general(wu_ref[...], final, NT, preferred_element_type=F32)
        update = update * live_ref[...]
        near, far = update[:, : atoms // 2], update[:, atoms // 2 :]
        keep_ref[s] = jnp.where(mine, near, far)
        send_ref[s] = jnp.where(mine, far, near)


def decode(col, left, own, right, pick, window, cond, scale, shift, bias, live, weights):
    samples = own.shape[0]
    atoms = window.shape[0] * WQ
    outputs = weights[-1].shape[0]
    vmem = pl.BlockSpec(memory_space=pltpu.VMEM)
    return pl.pallas_call(
        atom_kernel,
        in_specs=[pl.BlockSpec(memory_space=pltpu.SMEM)] + [vmem] * (10 + len(weights)),
        out_shape=[of((samples, outputs, atoms // 2), F32)] * 2,
        name="decode",
    )(col, left, own, right, pick, window, cond, scale, shift, bias, live, *weights)


def shards(
    tokens_in,
    cond_single,
    token_mask,
    pair_cond,
    w_pair,
    w_scale,
    w_shift,
    w_outgate,
    w_query,
    w_key,
    w_value,
    w_gate,
    w_out,
    atom_cond,
    atom_token,
    window_start,
    atom_mask,
    atom_pair,
    w_token_atom,
    w_ascale,
    w_ashift,
    w_aquery,
    w_akey,
    w_avalue,
    w_agate,
    w_aout,
    w_apair,
    w_update,
):
    samples, rows, width = tokens_in.shape
    count = lax.axis_size("row")
    local = samples // lax.axis_size("col")
    row, col = lax.axis_index("row"), lax.axis_index("col")
    col_index = col.astype(jnp.int32).reshape(1)
    keys = count * rows

    def swap(array):
        return lax.ppermute(array, "col", [(0, 1), (1, 0)])

    def in_order(array, axis):
        other = swap(array)
        return jnp.where(
            col == 0,
            jnp.concatenate([array, other], axis=axis),
            jnp.concatenate([other, array], axis=axis),
        )

    half = count // 2
    ring = list(range(0, count, 2)) + list(range(count - 1, 0, -2))
    forward = [(ring[p], ring[(p + 1) % count]) for p in range(count)]
    backward = [(b, a) for a, b in forward]
    position = jnp.where(row % 2 == 0, row // 2, half + (count - 1 - row) // 2)
    steps = [0]
    for k in range(1, half + 1):
        steps += [k, -k] if k < half else [k]
    source = (position - jnp.array(steps, jnp.int32)) % count
    source = jnp.where(source < half, 2 * source, count - 1 - 2 * (source - half))
    place = ((source - col * half) % count).astype(jnp.int32)

    slot = (row - col * half) % count
    lane = jnp.arange(keys, dtype=jnp.int32)
    valid = jnp.where(lane // rows == slot, jnp.tile(token_mask, count), 0).astype(BF16)
    valid_width = min(keys, 512)
    valid = valid.reshape(keys // valid_width, valid_width)
    valid = jnp.pad(valid, ((0, 8 - valid.shape[0]), (0, width - valid_width)))

    block = mix(col_index, tokens_in, cond_single, w_scale, w_shift, valid, local)

    near_bias = pair_bias_of(pair_cond, w_pair)
    far_bias = swap(near_bias)
    key_weights = (w_key, swap(w_key), w_value, swap(w_value))

    blocks = [block]
    held = project_kv(place, 0, [block], key_weights, None, local, rows, keys)
    ahead = behind = block
    for k in range(1, half + 1):
        ahead = lax.ppermute(ahead, "row", forward)
        arrived = [ahead]
        if k < half:
            behind = lax.ppermute(behind, "row", backward)
            arrived.append(behind)
        held = project_kv(place, len(blocks), arrived, key_weights, held, local, rows, keys)
        blocks += arrived

    query, gate, out_gate = project_q(
        block, (w_query, swap(w_query), w_gate, swap(w_gate)), cond_single, w_outgate, local * rows
    )

    atoms = atom_cond.shape[0]
    windows = window_start.shape[0]
    chip = 2 * atoms
    first = row * chip
    own_first = first + col * atoms
    atom_index = own_first + jnp.arange(atoms, dtype=jnp.int32)
    window_index = own_first // WQ + jnp.arange(windows, dtype=jnp.int32)
    ints = jnp.stack(
        [
            atom_token - atom_index // PER_TOKEN,
            atom_mask,
            jnp.pad(window_start - window_index * WQ, (0, atoms - windows)),
        ]
    )
    ints = jnp.pad(ints, ((0, 5), (0, 0))).astype(BF16)
    packed = jnp.concatenate([atom_cond, ints], axis=0)
    packed_other = swap(packed)
    lower = jnp.where(col == 0, packed, packed_other)
    upper = jnp.where(col == 0, packed_other, packed)
    chip_cond = jnp.concatenate([lower[:atoms], upper[:atoms]], axis=0)
    chip_ints = jnp.concatenate([lower[atoms:], upper[atoms:]], axis=1)
    top = jnp.pad(chip_ints[:1, :HALO], ((0, 7), (0, atoms - HALO)))
    bottom = jnp.pad(chip_ints[:1, chip - HALO :], ((0, 7), (0, atoms - HALO)))
    top = jnp.concatenate([chip_cond[:HALO], top], axis=0)
    bottom = jnp.concatenate([chip_cond[chip - HALO :], bottom], axis=0)
    up = [(i, i + 1) for i in range(count - 1)]
    down = [(i + 1, i) for i in range(count - 1)]
    before = lax.ppermute(bottom, "row", up)
    after = lax.ppermute(top, "row", down)
    cond_wide = jnp.concatenate([before[:HALO], chip_cond, after[:HALO]], axis=0)
    delta = jnp.concatenate(
        [before[HALO, :HALO], chip_ints[0], after[HALO, :HALO]], axis=0
    ).astype(jnp.int32)
    extent = chip + 2 * HALO
    wide_index = first - HALO + jnp.arange(extent, dtype=jnp.int32)
    token = delta + lax.shift_right_arithmetic(wide_index, 3) - (row - 1) * rows
    pick = (token[:, None] == jnp.arange(3 * rows, dtype=jnp.int32)[None, :]).astype(BF16)
    live = chip_ints[1:2].astype(F32)
    chip_windows = 2 * windows
    order = jnp.arange(chip_windows, dtype=jnp.int32)
    shifts = jnp.concatenate([lower[atoms + 2, :windows], upper[atoms + 2, :windows]], axis=0)
    base = jnp.clip(order * WQ - WQ, 0, extent - SPAN)
    offset = shifts.astype(jnp.int32) + order * WQ + HALO - base
    window = (
        offset[:, None, None] + jnp.arange(WK, dtype=jnp.int32)[None, :, None]
        == jnp.arange(SPAN, dtype=jnp.int32)[None, None, :]
    ).astype(BF16)
    atom_scale, atom_shift = atom_cond_of(cond_wide, w_ascale, w_ashift)
    atom_bias = in_order(atom_bias_of(atom_pair, w_apair), 0)

    tokens, projected = attend(
        col_index, query, *held, near_bias, far_bias, gate, out_gate, tokens_in,
        (w_out, swap(w_out)), w_token_atom, blocks, valid_width,
    )
    left = lax.ppermute(projected, "row", up)
    right = lax.ppermute(projected, "row", down)
    tokens_out = in_order(tokens, 0)
    keep, send = decode(
        col_index, left, projected, right, pick, window, cond_wide, atom_scale, atom_shift, atom_bias,
        live, (w_aquery, w_akey, w_avalue, w_agate, w_aout, w_update),
    )
    theirs = swap(send)
    atom_update = jnp.where(
        col == 0,
        jnp.concatenate([keep, theirs], axis=0),
        jnp.concatenate([theirs, keep], axis=0),
    )
    return (tokens_out, atom_update)


def solution(mesh):
    return jax.shard_map(
        shards,
        mesh=mesh,
        in_specs=(
            P("groups", "row", None),
            P(("groups", "row"), None),
            P(("groups", "row")),
            P(("groups", "row"), "col", None),
            P(),
            P(),
            P(),
            P(),
            P(None, "col"),
            P(None, "col"),
            P(None, "col"),
            P(None, "col"),
            P("col", None),
            P(("groups", "row", "col"), None),
            P(("groups", "row", "col")),
            P(("groups", "row", "col")),
            P(("groups", "row", "col")),
            P(("groups", "row", "col"), None, None, None),
            P(),
            P(),
            P(),
            P(),
            P(),
            P(),
            P(),
            P(),
            P(),
            P(),
        ),
        out_specs=(P("groups", "row", None), P("groups", None, ("row", "col"))),
        check_vma=False,
    )
```

time: 170 us -> 105 us (0.62)
  Pallas kernels: 0 us -> 53.2 us
  waiting for transfers between devices: 50.8 us -> 8.68 us
  local copies, waits for them, and re-layouts: 28.7 us -> 5.57 us
  matrix products: 21.5 us -> 0 us
  blocking collectives: 19.7 us -> 0 us
  between operations: 15.7 us -> 0.93 us
  starting transfers between devices: 16 us -> 27.5 us
  other arithmetic: 16.6 us -> 7.34 us
    pallas_call x0 -> x12, Pallas kernels: none -> 53.2 us  [the longest x5 20.6 us: project_kv(): pl.pallas_call(functools.partial(kv_kernel, count, aliased), grid_spec=pl...]
    all_gather x1 -> x0, waiting for transfers between devices: 26.3 us -> none  [shards(): kv_piece = lax.all_gather(stacked, 'row', axis=2, tiled=True)]
    dot_general x21 -> x0, matrix products: 21.5 us -> none  [the longest x1 2.82 us: shards(): jnp.einsum('sqe,ed->sqd', gated, w_out, preferred_element_type=jnp.float32)]
    unnamed x1 -> x0, blocking collectives: 19.7 us -> none
    psum x1 -> x0, waiting for transfers between devices: 17 us -> none  [shards(): lax.psum(partial_value.astype(jnp.bfloat16), 'col').astype(jnp.float32)]
    ppermute x4 -> x21, starting transfers between devices: 12.4 us -> 27.5 us  [the longest x10 9.89 us: swap(): return lax.ppermute(array, 'col', [(0, 1), (1, 0)])]
    slice x4 -> x10, local copies, waits for them, and re-layouts: 7.71 us -> 0.1 us  [the longest x1 0.07 us: shards(): bottom = jnp.pad(chip_ints[:1, chip - HALO:], ((0, 7), (0, atoms - HALO)))]
    reduce_sum x13 -> x0, other arithmetic: 7.35 us -> none  [the longest x5 2.57 us: layer_norm(): centred = inputs - jnp.mean(inputs, axis=-1, keepdims=True)]
  transfers between devices with their start and end apart: 7 -> 21, of which waited for: 5 -> 5; matrix products, arithmetic and copies ran while one was open for 8% -> 8% of each run, Pallas kernels for 0% -> 48%
where the time goes in v1:
time: 105 us; the launch traced here: 103 us
  Pallas kernels  53.2 us (51%)
  starting transfers between devices  27.5 us (26%)
  waiting for transfers between devices  8.68 us (8%)
  other arithmetic  7.34 us (7%)
  local copies, waits for them, and re-layouts  5.57 us (5%)
    pallas_call x5, Pallas kernels, project_kv(): pl.pallas_call(functools.partial(kv_kernel, count, aliased), grid_spec=pl...  20.6 us
    pallas_call x1, Pallas kernels, decode(): pl.pallas_call(atom_kernel, in_specs=[pl.BlockSpec(memory_space=pltpu.SME...  11.7 us
    ppermute x10, starting transfers between devices, swap(): return lax.ppermute(array, 'col', [(0, 1), (1, 0)])  9.89 us
    ppermute x4, starting transfers between devices, shards(): ahead = lax.ppermute(ahead, 'row', forward)  8.27 us
    pallas_call x1, Pallas kernels, attend(): pl.pallas_call(functools.partial(attend_kernel, len(blocks), valid_width)...  7.58 us
    ppermute x3, waiting for transfers between devices, shards(): behind = lax.ppermute(behind, 'row', backward)  4.55 us
    ppermute x1, starting transfers between devices, shards(): before = lax.ppermute(bottom, 'row', up)  3.59 us
    pallas_call x1, Pallas kernels, project_q(): pl.pallas_call(functools.partial(query_kernel, HEAD ** (-0.5)), grid=(1,)...  3.45 us
  transfers between devices with their start and end apart: 21, of which 5 were waited for; matrix products, arithmetic and copies ran while one was open for 8% of the time, Pallas kernels for 48%

profile of v1, /device:TPU:1, one launch (start us, length us, event | category | flops | bytes accessed | tf_op | source)
XLA Modules:
  0.0 103.3 jit_solution(14099705787696254563)
XLA Ops:
  0.6 0.0 copy-start
  0.7 0.7 tile.4
  1.4 0.1 tile.10
  1.5 0.6 pad.21.valid_ref
  2.1 3.1 %mix.1.block_ref.refs_0_ = bf16[136,768]{1,0:T(8,128)(2,1)} custom-call(s32[1]{0:T(128)} %bitcast.col_ref, bf16[8,32,768]{2,1,0:T(8,128)(2,1)} %tok_ref.3, bf16[32,768]{1,0:T(8,128)(2,1)} %cond_ref.3, bf16[768,768]{1,0:T(8,128)(2,1)} %scale_ref.2, bf16[768,768]{1,0:T(8,128)(2,1)} %shift_ref.2, bf16[8,768]{1,0:T(8,128)(2,1)} %pad.21.valid_ref), custom_call_target="tpu_custom_call" | custom-call | tf_op jit(solution)/shard_map/mix/pallas_call | solution.py:57
  5.3 2.1 %collective-permute-start.2 = (bf16[136,768]{1,0:T(8,128)(2,1)}, bf16[136,768]{1,0:T(8,128)(2,1)S(1)}, u32[]{:S(2)}, u32[]{:S(2)}) collective-permute-start(bf16[136,768]{1,0:T(8,128)(2,1)} %mix.1.block_ref.refs_0_), channel_id=1, source_target_pairs={{0,4},{4,8},{8,12},{12,14},{14,10},{10,6},{6,2},{2,0},{1,5},{5,9},... | collective-permute-start | bytes 626696 | tf_op jit(solution)/shard_map/ppermute | solution.py:452
  7.4 0.0 collective-permute-start.8
  7.4 1.0 collective-permute-start.6
  8.4 0.1 collective-permute-start.16
  8.6 0.6 and_select_fusion.2.place_ref
  9.2 0.7 copy.41.w_ref
  9.9 2.6 %pair_bias.1.bl_ref = f32[16,32,128]{2,1,0:T(8,128)} custom-call(bf16[32,128,128]{2,1,0:T(8,128)(2,1)} %pair_ref.2, bf16[16,128]{1,0:T(8,128)(2,1)} %bitcast.16), custom_call_target="tpu_custom_call" | custom-call | tf_op jit(solution)/shard_map/pair_bias/pallas_call | solution.py:153
  12.5 2.2 %atom_bias.1 = f32[4,128,128]{2,1,0:T(8,128)} custom-call(f32[16,4]{1,0:T(8,128)} %copy.41.w_ref, bf16[4,16,32,128]{3,2,1,0:T(8,128)(2,1)} %pair_ref.3), custom_call_target="tpu_custom_call" | custom-call | tf_op jit(solution)/shard_map/atom_bias/pallas_call | solution.py:285
  14.6 0.1 slice.69
  14.8 3.6 %collective-permute-start.17 = (bf16[72,128]{1,0:T(8,128)(2,1)S(1)}, bf16[72,128]{1,0:T(8,128)(2,1)S(1)}, u32[]{:S(2)}, u32[]{:S(2)}) collective-permute-start(bf16[72,128]{1,0:T(8,128)(2,1)S(1)} %fusion.4), channel_id=1, source_target_pairs={{0,2},{2,4},{4,6},{6,8},{8,10},{10,12},{12,14},{1,3},{3,5},{5,7},{... | collective-permute-start | bytes 55304 | tf_op jit(solution)/shard_map/ppermute | solution.py:491
  18.4 1.3 %collective-permute-start.18 = (bf16[72,128]{1,0:T(8,128)(2,1)S(1)}, bf16[72,128]{1,0:T(8,128)(2,1)S(1)}, u32[]{:S(2)}, u32[]{:S(2)}) collective-permute-start(bf16[72,128]{1,0:T(8,128)(2,1)S(1)} %fusion.5), channel_id=1, source_target_pairs={{2,0},{4,2},{6,4},{8,6},{10,8},{12,10},{14,12},{3,1},{5,3},{7,5},{... | collective-permute-start | bytes 55304 | tf_op jit(solution)/shard_map/ppermute | solution.py:492
  19.7 0.1 fusion.18
  19.8 0.1 iota_add_fusion
  19.8 0.0 collective-permute-done.2.refs_0_.refs_1_
  19.8 3.0 %collective-permute-start.3 = (bf16[136,768]{1,0:T(8,128)(2,1)S(1)}, bf16[136,768]{1,0:T(8,128)(2,1)S(1)}, u32[]{:S(2)}, u32[]{:S(2)}) collective-permute-start(bf16[136,768]{1,0:T(8,128)(2,1)S(1)} %collective-permute-done.2.refs_0_.refs_1_), channel_id=1, source_target_pairs={{0,4},{4,8},{8,12},{12,14},{14,10},{10,6},{6,2},{2,0},{1,5},{5,9},... | collective-permute-start | bytes 626696 | tf_op jit(solution)/shard_map/ppermute | solution.py:452
  22.9 1.0 fusion.win_ref
  23.9 1.4 %collective-permute-start.7 = (bf16[768,384]{1,0:T(8,128)(2,1)S(1)}, bf16[768,384]{1,0:T(8,128)(2,1)S(1)}, u32[]{:S(2)}, u32[]{:S(2)}) collective-permute-start(bf16[768,384]{1,0:T(8,128)(2,1)S(1)} %copy-done.1), channel_id=1, source_target_pairs={{0,1},{1,0},{2,3},{3,2},{4,5},{5,4},{6,7},{7,6},{8,9},{9,8},{10,11... | collective-permute-start | bytes 1769480 | tf_op jit(solution)/shard_map/ppermute | solution.py:413
  25.3 0.1 collective-permute-start
  25.3 0.6 fusion.12
  26.0 0.5 collective-permute-start.1
  26.5 0.2 collective-permute-done.3.refs_0_.refs_3_
  26.7 1.1 %collective-permute-start.9 = (bf16[136,768]{1,0:T(8,128)(2,1)S(1)}, bf16[136,768]{1,0:T(8,128)(2,1)S(1)}, u32[]{:S(2)}, u32[]{:S(2)}) collective-permute-start(bf16[136,768]{1,0:T(8,128)(2,1)S(1)} %collective-permute-done.8.refs_1_.refs_2_), channel_id=1, source_target_pairs={{4,0},{8,4},{12,8},{14,12},{10,14},{6,10},{2,6},{0,2},{5,1},{9,5},... | collective-permute-start | bytes 626696 | tf_op jit(solution)/shard_map/ppermute | solution.py:455
  27.7 4.5 %collective-permute-done.9.refs_1_.refs_4_ = bf16[136,768]{1,0:T(8,128)(2,1)S(1)} collective-permute-done((bf16[136,768]{1,0:T(8,128)(2,1)S(1)}, bf16[136,768]{1,0:T(8,128)(2,1)S(1)}, u32[]{:S(2)}, u32[]{:S(2)}) %collective-permute-start.9) | collective-permute-done | bytes 208928 | tf_op jit(solution)/shard_map/ppermute | solution.py:455
  32.3 2.4 %collective-permute-start.12 = (bf16[384,768]{1,0:T(8,128)(2,1)}, bf16[384,768]{1,0:T(8,128)(2,1)}, u32[]{:S(2)}, u32[]{:S(2)}) collective-permute-start(bf16[384,768]{1,0:T(8,128)(2,1)} %wol_ref.1), channel_id=1, source_target_pairs={{0,1},{1,0},{2,3},{3,2},{4,5},{5,4},{6,7},{7,6},{8,9},{9,8},{10,11... | collective-permute-start | bytes 1769480 | tf_op jit(solution)/shard_map/ppermute | solution.py:413
  34.7 1.6 %collective-permute-start.4 = (bf16[136,768]{1,0:T(8,128)(2,1)S(1)}, bf16[136,768]{1,0:T(8,128)(2,1)S(1)}, u32[]{:S(2)}, u32[]{:S(2)}) collective-permute-start(bf16[136,768]{1,0:T(8,128)(2,1)S(1)} %collective-permute-done.3.refs_0_.refs_3_), channel_id=1, source_target_pairs={{0,4},{4,8},{8,12},{12,14},{14,10},{10,6},{6,2},{2,0},{1,5},{5,9},... | collective-permute-start | bytes 626696 | tf_op jit(solution)/shard_map/ppermute | solution.py:452
  36.3 0.6 pad_maximum_fusion.cond_ref
  36.9 0.0 collective-permute-done.7.refs_4_.refs_5_
  36.9 0.4 collective-permute-start.11
  37.3 0.2 collective-permute-start.19
  37.5 0.1 add_subtract_fusion
  37.6 2.0 %atom_cond.1 = (f32[384,128]{1,0:T(8,128)}, f32[384,128]{1,0:T(8,128)}) custom-call(bf16[384,128]{1,0:T(8,128)(2,1)} %pad_maximum_fusion.cond_ref, bf16[128,128]{1,0:T(8,128)(2,1)} %scale_ref.3, bf16[128,128]{1,0:T(8,128)(2,1)} %shift_ref.3), custom_call_target="tpu_custom_call" | custom-call | tf_op jit(solution)/shard_map/atom_cond/pallas_call | solution.py:300
  39.6 0.0 collective-permute-done.1.gr_ref
  39.6 0.0 collective-permute-start.10
  39.6 1.8 %collective-permute-done.4.refs_0_.refs_5_ = bf16[136,768]{1,0:T(8,128)(2,1)S(1)} collective-permute-done((bf16[136,768]{1,0:T(8,128)(2,1)S(1)}, bf16[136,768]{1,0:T(8,128)(2,1)S(1)}, u32[]{:S(2)}, u32[]{:S(2)}) %collective-permute-start.4) | collective-permute-done | bytes 208928 | tf_op jit(solution)/shard_map/ppermute | solution.py:452
  41.4 1.6 %collective-permute-start.5 = (bf16[136,768]{1,0:T(8,128)(2,1)S(1)}, bf16[136,768]{1,0:T(8,128)(2,1)S(1)}, u32[]{:S(2)}, u32[]{:S(2)}) collective-permute-start(bf16[136,768]{1,0:T(8,128)(2,1)S(1)} %collective-permute-done.4.refs_0_.refs_5_), channel_id=1, source_target_pairs={{0,4},{4,8},{8,12},{12,14},{14,10},{10,6},{6,2},{2,0},{1,5},{5,9},... | collective-permute-start | bytes 626696 | tf_op jit(solution)/shard_map/ppermute | solution.py:452
  42.9 0.8 fusion.1.pick_ref
  43.7 3.6 %project_kv.5 = (bf16[4,256,768]{2,1,0:T(8,128)(2,1)}, bf16[4,256,768]{2,1,0:T(8,128)(2,1)}) custom-call(s32[8]{0:T(128)} %and_select_fusion.2.place_ref, bf16[136,768]{1,0:T(8,128)(2,1)} %mix.1.block_ref.refs_0_, bf16[768,384]{1,0:T(8,128)(2,1)} %refs_1_.3, bf16[768,384]{1,0:T(8,128)(2,1)} %copy-done.2, bf16[768,384]{1,0:T(8,128)(2,1)} %refs_3_.3, ...), custom_call_target="tpu_custom_call" | custom-call | tf_op jit(solution)/shard_map/project_kv/pallas_call | solution.py:99
  47.4 4.5 %project_kv.6 = (bf16[4,256,768]{2,1,0:T(8,128)(2,1)}, bf16[4,256,768]{2,1,0:T(8,128)(2,1)}) custom-call(s32[8]{0:T(128)} %and_select_fusion.2.place_ref, bf16[136,768]{1,0:T(8,128)(2,1)} %copy-done.7, bf16[136,768]{1,0:T(8,128)(2,1)} %copy-done.8, bf16[768,384]{1,0:T(8,128)(2,1)} %refs_1_.3, ...), custom_call_target="tpu_custom_call", output_to_operand_aliasing={{0}: (7, {}), {1}: (8, {})} | custom-call | tf_op jit(solution)/shard_map/project_kv/pallas_call | solution.py:99
  51.8 4.4 %project_kv.7 = (bf16[4,256,768]{2,1,0:T(8,128)(2,1)}, bf16[4,256,768]{2,1,0:T(8,128)(2,1)}) custom-call(s32[8]{0:T(128)} %and_select_fusion.2.place_ref, bf16[136,768]{1,0:T(8,128)(2,1)} %copy-done.9, bf16[136,768]{1,0:T(8,128)(2,1)} %copy-done.10, bf16[768,384]{1,0:T(8,128)(2,1)} %refs_1_.3, ...), custom_call_target="tpu_custom_call", output_to_operand_aliasing={{0}: (7, {}), {1}: (8, {})} | custom-call | tf_op jit(solution)/shard_map/project_kv/pallas_call | solution.py:99
  56.2 3.4 %project_q.1 = (bf16[128,768]{1,0:T(8,128)(2,1)}, f32[128,768]{1,0:T(8,128)}, f32[32,768]{1,0:T(8,128)}) custom-call(bf16[136,768]{1,0:T(8,128)(2,1)} %mix.1.block_ref.refs_0_, bf16[768,384]{1,0:T(8,128)(2,1)} %ql_ref.1, bf16[768,384]{1,0:T(8,128)(2,1)} %collective-permute-done.qr_ref, bf16[768,384]{1,0:T(8,128)(2,1)} %gl_ref.1, ...), custom_call_target="tpu_custom_call" | custom-call | tf_op jit(solution)/shard_map/project_q/pallas_call | solution.py:129
  59.7 0.7 copy-done.12
  60.4 4.4 %project_kv.8 = (bf16[4,256,768]{2,1,0:T(8,128)(2,1)}, bf16[4,256,768]{2,1,0:T(8,128)(2,1)}) custom-call(s32[8]{0:T(128)} %and_select_fusion.2.place_ref, bf16[136,768]{1,0:T(8,128)(2,1)} %copy-done.11, bf16[136,768]{1,0:T(8,128)(2,1)} %copy-done.12, bf16[768,384]{1,0:T(8,128)(2,1)} %refs_1_.3, ...), custom_call_target="tpu_custom_call", output_to_operand_aliasing={{0}: (7, {}), {1}: (8, {})} | custom-call | tf_op jit(solution)/shard_map/project_kv/pallas_call | solution.py:99
  64.8 0.0 collective-permute-done.5.refs_0_.refs_7_
  64.8 0.7 copy-done.6
  65.5 3.7 %project_kv.9 = (bf16[4,256,768]{2,1,0:T(8,128)(2,1)}, bf16[4,256,768]{2,1,0:T(8,128)(2,1)}) custom-call(s32[8]{0:T(128)} %and_select_fusion.2.place_ref, bf16[136,768]{1,0:T(8,128)(2,1)} %copy-done.6, bf16[768,384]{1,0:T(8,128)(2,1)} %refs_1_.3, bf16[768,384]{1,0:T(8,128)(2,1)} %copy-done.2, ...), custom_call_target="tpu_custom_call", output_to_operand_aliasing={{0}: (6, {}), {1}: (7, {})} | custom-call | tf_op jit(solution)/shard_map/project_kv/pallas_call | solution.py:99
  69.1 0.7 copy-done.13
  69.9 7.6 %attend.1 = (bf16[4,32,768]{2,1,0:T(8,128)(2,1)}, bf16[4,32,128]{2,1,0:T(8,128)(2,1)}) custom-call(s32[1]{0:T(128)} %bitcast.col_ref, bf16[128,768]{1,0:T(8,128)(2,1)} %get-tuple-element.21.q_ref, bf16[4,256,768]{2,1,0:T(8,128)(2,1)} %get-tuple-element.30.k_ref, bf16[4,256,768]{2,1,0:T(8,128)(2,1)} %get-tuple-element.31.v_ref, ...), custom_call_target="tpu_custom_call" | custom-call | tf_op jit(solution)/shard_map/attend/pallas_call | solution.py:236
  77.4 1.9 %collective-permute-start.14 = (bf16[4,32,128]{2,1,0:T(8,128)(2,1)}, bf16[4,32,128]{2,1,0:T(8,128)(2,1)S(1)}, u32[]{:S(2)}, u32[]{:S(2)}) collective-permute-start(bf16[4,32,128]{2,1,0:T(8,128)(2,1)} %get-tuple-element.35.own_ref), channel_id=1, source_target_pairs={{0,2},{2,4},{4,6},{6,8},{8,10},{10,12},{12,14},{1,3},{3,5},{5,7},{... | collective-permute-start | bytes 98312 | tf_op jit(solution)/shard_map/ppermute | solution.py:518
  79.4 1.5 %collective-permute-start.15 = (bf16[4,32,128]{2,1,0:T(8,128)(2,1)}, bf16[4,32,128]{2,1,0:T(8,128)(2,1)S(1)}, u32[]{:S(2)}, u32[]{:S(2)}) collective-permute-start(bf16[4,32,128]{2,1,0:T(8,128)(2,1)} %get-tuple-element.35.own_ref), channel_id=1, source_target_pairs={{2,0},{4,2},{6,4},{8,6},{10,8},{12,10},{14,12},{3,1},{5,3},{7,5},{... | collective-permute-start | bytes 98312 | tf_op jit(solution)/shard_map/ppermute | solution.py:519
  80.9 1.5 %collective-permute-start.13 = (bf16[4,32,768]{2,1,0:T(8,128)(2,1)}, bf16[4,32,768]{2,1,0:T(8,128)(2,1)S(1)}, u32[]{:S(2)}, u32[]{:S(2)}) collective-permute-start(bf16[4,32,768]{2,1,0:T(8,128)(2,1)} %get-tuple-element.34), channel_id=1, source_target_pairs={{0,1},{1,0},{2,3},{3,2},{4,5},{5,4},{6,7},{7,6},{8,9},{9,8},{10,11... | collective-permute-start | bytes 589832 | tf_op jit(solution)/shard_map/ppermute | solution.py:413
  82.4 1.9 %maximum_select_fusion.bias_ref = f32[8,128,128]{2,1,0:T(8,128)} fusion(f32[4,128,128]{2,1,0:T(8,128)} %collective-permute-done.19, f32[4,128,128]{2,1,0:T(8,128)S(1)} %copy-done.5, pred[]{:T(512)S(6)} %eq.55), kind=kLoop, calls=%fused_computation.2 | loop fusion | flops 393216 | bytes 1048577 | tf_op jit(solution)/shard_map/jit(_where)/select_n | solution.py:417
  84.3 1.1 %collective-permute-done.15.right_ref = bf16[4,32,128]{2,1,0:T(8,128)(2,1)S(1)} collective-permute-done((bf16[4,32,128]{2,1,0:T(8,128)(2,1)}, bf16[4,32,128]{2,1,0:T(8,128)(2,1)S(1)}, u32[]{:S(2)}, u32[]{:S(2)}) %collective-permute-start.15) | collective-permute-done | bytes 32800 | tf_op jit(solution)/shard_map/ppermute | solution.py:519
  85.4 0.6 copy-done.17
  86.0 11.7 %decode.1 = (f32[4,3,128]{2,1,0:T(4,128)}, f32[4,3,128]{2,1,0:T(4,128)}) custom-call(s32[1]{0:T(128)} %bitcast.col_ref, bf16[4,32,128]{2,1,0:T(8,128)(2,1)} %copy-done.16, bf16[4,32,128]{2,1,0:T(8,128)(2,1)} %get-tuple-element.35.own_ref, bf16[4,32,128]{2,1,0:T(8,128)(2,1)} %copy-done.17, bf16[384,96]{1,0:T(8,128)(2,1)} %fusion.1.pick_ref, ...), custom_call_target="tpu_custom_call" | custom-call | tf_op jit(solution)/shard_map/decode/pallas_call | solution.py:367
  97.7 2.3 %collective-permute-start.20 = (f32[4,3,128]{2,1,0:T(4,128)}, f32[4,3,128]{2,1,0:T(4,128)S(1)}, u32[]{:S(2)}, u32[]{:S(2)}) collective-permute-start(f32[4,3,128]{2,1,0:T(4,128)} %get-tuple-element.39), channel_id=1, source_target_pairs={{0,1},{1,0},{2,3},{3,2},{4,5},{5,4},{6,7},{7,6},{8,9},{9,8},{10,11... | collective-permute-start | bytes 18440 | tf_op jit(solution)/shard_map/ppermute | solution.py:413
  100.1 1.0 %collective-permute-done.20 = f32[4,3,128]{2,1,0:T(4,128)S(1)} collective-permute-done((f32[4,3,128]{2,1,0:T(4,128)}, f32[4,3,128]{2,1,0:T(4,128)S(1)}, u32[]{:S(2)}, u32[]{:S(2)}) %collective-permute-start.20) | collective-permute-done | bytes 6176 | tf_op jit(solution)/shard_map/ppermute | solution.py:413
  101.1 0.8 maximum_select_fusion.2
  101.9 0.6 copy.42
  102.5 0.8 maximum_select_fusion.1
  (75 shorter events, 0.2 us)
Async XLA Ops:
  0.6 6.7 %copy-start = (bf16[768,384]{1,0:T(8,128)(2,1)S(1)}, bf16[768,384]{1,0:T(8,128)(2,1)}, u32[]{:S(2)}) copy-start(bf16[768,384]{1,0:T(8,128)(2,1)} %refs_1_.3) | copy-start | bytes 1769476
  0.6 7.7 %copy-start.22 = (s32[4]{0:T(128)S(1)}, s32[4]{0:T(128)}, u32[]{:S(2)}) copy-start(s32[4]{0:T(128)} %param.44) | copy-start | bytes 52
  0.7 7.7 %copy-start.20 = (s32[128]{0:T(128)S(1)}, s32[128]{0:T(128)}, u32[]{:S(2)}) copy-start(s32[128]{0:T(128)} %param.43) | copy-start | bytes 1540
  0.7 7.7 %copy-start.19 = (s32[128]{0:T(128)S(1)}, s32[128]{0:T(128)}, u32[]{:S(2)}) copy-start(s32[128]{0:T(128)} %param.45) | copy-start | bytes 1540
  0.7 7.7 %copy-start.15 = (bf16[128,128]{1,0:T(8,128)(2,1)S(1)}, bf16[128,128]{1,0:T(8,128)(2,1)}, u32[]{:S(2)}) copy-start(bf16[128,128]{1,0:T(8,128)(2,1)} %param.42) | copy-start | bytes 98308
  2.1 6.4 %copy-start.21 = (s32[8]{0:T(128)S(1)}, s32[8]{0:T(128)}, u32[]{:S(2)}) copy-start(s32[8]{0:T(128)} %constant.139) | copy-start | bytes 100
  2.1 7.0 %copy-start.18 = (bf16[16,4]{0,1:T(4,128)(2,1)S(1)}, bf16[16,4]{0,1:T(4,128)(2,1)}, u32[]{:S(2)}) copy-start(bf16[16,4]{0,1:T(4,128)(2,1)} %param.55) | copy-start | bytes 388
  5.3 14.6 %collective-permute-start.2 = (bf16[136,768]{1,0:T(8,128)(2,1)}, bf16[136,768]{1,0:T(8,128)(2,1)S(1)}, u32[]{:S(2)}, u32[]{:S(2)}) collective-permute-start(bf16[136,768]{1,0:T(8,128)(2,1)} %mix.1.block_ref.refs_0_), channel_id=1, source_target_pairs={{0,4},{4,8},{8,12},{12,14},{14,10},{10,6},{6,2},{2,0},{1,5},{5,9},... | collective-permute-start | bytes 626696 | tf_op jit(solution)/shard_map/ppermute | solution.py:452
  7.4 18.6 %collective-permute-start.8 = (bf16[136,768]{1,0:T(8,128)(2,1)}, bf16[136,768]{1,0:T(8,128)(2,1)S(1)}, u32[]{:S(2)}, u32[]{:S(2)}) collective-permute-start(bf16[136,768]{1,0:T(8,128)(2,1)} %mix.1.block_ref.refs_0_), channel_id=1, source_target_pairs={{4,0},{8,4},{12,8},{14,12},{10,14},{6,10},{2,6},{0,2},{5,1},{9,5},... | collective-permute-start | bytes 626696 | tf_op jit(solution)/shard_map/ppermute | solution.py:455
  7.4 27.3 %collective-permute-start.6 = (bf16[768,384]{1,0:T(8,128)(2,1)S(1)}, bf16[768,384]{1,0:T(8,128)(2,1)S(1)}, u32[]{:S(2)}, u32[]{:S(2)}) collective-permute-start(bf16[768,384]{1,0:T(8,128)(2,1)S(1)} %copy-done), channel_id=1, source_target_pairs={{0,1},{1,0},{2,3},{3,2},{4,5},{5,4},{6,7},{7,6},{8,9},{9,8},{10,11... | collective-permute-start | bytes 1769480 | tf_op jit(solution)/shard_map/ppermute | solution.py:413
  8.3 15.6 %copy-start.1 = (bf16[768,384]{1,0:T(8,128)(2,1)S(1)}, bf16[768,384]{1,0:T(8,128)(2,1)}, u32[]{:S(2)}) copy-start(bf16[768,384]{1,0:T(8,128)(2,1)} %refs_3_.3) | copy-start | bytes 1769476
  8.4 6.2 %collective-permute-start.16 = (bf16[136,128]{1,0:T(8,128)(2,1)S(1)}, bf16[136,128]{1,0:T(8,128)(2,1)S(1)}, u32[]{:S(2)}, u32[]{:S(2)}) collective-permute-start(bf16[136,128]{1,0:T(8,128)(2,1)S(1)} %pad_maximum_fusion.1), channel_id=1, source_target_pairs={{0,1},{1,0},{2,3},{3,2},{4,5},{5,4},{6,7},{7,6},{8,9},{9,8},{10,11... | collective-permute-start | bytes 104456 | tf_op jit(solution)/shard_map/ppermute | solution.py:413
  12.5 24.5 %copy-start.4 = (f32[16,32,128]{2,1,0:T(8,128)S(1)}, f32[16,32,128]{2,1,0:T(8,128)}, u32[]{:S(2)}) copy-start(f32[16,32,128]{2,1,0:T(8,128)} %pair_bias.1.bl_ref) | copy-start | bytes 786436
  14.8 9.1 %collective-permute-start.17 = (bf16[72,128]{1,0:T(8,128)(2,1)S(1)}, bf16[72,128]{1,0:T(8,128)(2,1)S(1)}, u32[]{:S(2)}, u32[]{:S(2)}) collective-permute-start(bf16[72,128]{1,0:T(8,128)(2,1)S(1)} %fusion.4), channel_id=1, source_target_pairs={{0,2},{2,4},{4,6},{6,8},{8,10},{10,12},{12,14},{1,3},{3,5},{5,7},{... | collective-permute-start | bytes 55304 | tf_op jit(solution)/shard_map/ppermute | solution.py:491
  18.4 6.9 %collective-permute-start.18 = (bf16[72,128]{1,0:T(8,128)(2,1)S(1)}, bf16[72,128]{1,0:T(8,128)(2,1)S(1)}, u32[]{:S(2)}, u32[]{:S(2)}) collective-permute-start(bf16[72,128]{1,0:T(8,128)(2,1)S(1)} %fusion.5), channel_id=1, source_target_pairs={{2,0},{4,2},{6,4},{8,6},{10,8},{12,10},{14,12},{3,1},{5,3},{7,5},{... | collective-permute-start | bytes 55304 | tf_op jit(solution)/shard_map/ppermute | solution.py:492
  19.8 27.5 %copy-start.7 = (bf16[136,768]{1,0:T(8,128)(2,1)}, bf16[136,768]{1,0:T(8,128)(2,1)S(1)}, u32[]{:S(2)}) copy-start(bf16[136,768]{1,0:T(8,128)(2,1)S(1)} %collective-permute-done.2.refs_0_.refs_1_) | copy-start | bytes 626692
  19.8 6.8 %collective-permute-start.3 = (bf16[136,768]{1,0:T(8,128)(2,1)S(1)}, bf16[136,768]{1,0:T(8,128)(2,1)S(1)}, u32[]{:S(2)}, u32[]{:S(2)}) collective-permute-start(bf16[136,768]{1,0:T(8,128)(2,1)S(1)} %collective-permute-done.2.refs_0_.refs_1_), channel_id=1, source_target_pairs={{0,4},{4,8},{8,12},{12,14},{14,10},{10,6},{6,2},{2,0},{1,5},{5,9},... | collective-permute-start | bytes 626696 | tf_op jit(solution)/shard_map/ppermute | solution.py:452
  23.9 13.0 %collective-permute-start.7 = (bf16[768,384]{1,0:T(8,128)(2,1)S(1)}, bf16[768,384]{1,0:T(8,128)(2,1)S(1)}, u32[]{:S(2)}, u32[]{:S(2)}) collective-permute-start(bf16[768,384]{1,0:T(8,128)(2,1)S(1)} %copy-done.1), channel_id=1, source_target_pairs={{0,1},{1,0},{2,3},{3,2},{4,5},{5,4},{6,7},{7,6},{8,9},{9,8},{10,11... | collective-permute-start | bytes 1769480 | tf_op jit(solution)/shard_map/ppermute | solution.py:413
  25.3 12.1 %collective-permute-start = (bf16[768,384]{1,0:T(8,128)(2,1)}, bf16[768,384]{1,0:T(8,128)(2,1)}, u32[]{:S(2)}, u32[]{:S(2)}) collective-permute-start(bf16[768,384]{1,0:T(8,128)(2,1)} %ql_ref.1), channel_id=1, source_target_pairs={{0,1},{1,0},{2,3},{3,2},{4,5},{5,4},{6,7},{7,6},{8,9},{9,8},{10,11... | collective-permute-start | bytes 1769480 | tf_op jit(solution)/shard_map/ppermute | solution.py:413
  26.0 21.4 %copy-start.8 = (bf16[136,768]{1,0:T(8,128)(2,1)}, bf16[136,768]{1,0:T(8,128)(2,1)S(1)}, u32[]{:S(2)}) copy-start(bf16[136,768]{1,0:T(8,128)(2,1)S(1)} %collective-permute-done.8.refs_1_.refs_2_) | copy-start | bytes 626692
  26.0 13.6 %collective-permute-start.1 = (bf16[768,384]{1,0:T(8,128)(2,1)}, bf16[768,384]{1,0:T(8,128)(2,1)}, u32[]{:S(2)}, u32[]{:S(2)}) collective-permute-start(bf16[768,384]{1,0:T(8,128)(2,1)} %gl_ref.1), channel_id=1, source_target_pairs={{0,1},{1,0},{2,3},{3,2},{4,5},{5,4},{6,7},{7,6},{8,9},{9,8},{10,11... | collective-permute-start | bytes 1769480 | tf_op jit(solution)/shard_map/ppermute | solution.py:413
  26.7 25.2 %copy-start.9 = (bf16[136,768]{1,0:T(8,128)(2,1)}, bf16[136,768]{1,0:T(8,128)(2,1)S(1)}, u32[]{:S(2)}) copy-start(bf16[136,768]{1,0:T(8,128)(2,1)S(1)} %collective-permute-done.3.refs_0_.refs_3_) | copy-start | bytes 626692
  26.7 5.6 %collective-permute-start.9 = (bf16[136,768]{1,0:T(8,128)(2,1)S(1)}, bf16[136,768]{1,0:T(8,128)(2,1)S(1)}, u32[]{:S(2)}, u32[]{:S(2)}) collective-permute-start(bf16[136,768]{1,0:T(8,128)(2,1)S(1)} %collective-permute-done.8.refs_1_.refs_2_), channel_id=1, source_target_pairs={{4,0},{8,4},{12,8},{14,12},{10,14},{6,10},{2,6},{0,2},{5,1},{9,5},... | collective-permute-start | bytes 626696 | tf_op jit(solution)/shard_map/ppermute | solution.py:455
  32.3 19.6 %copy-start.10 = (bf16[136,768]{1,0:T(8,128)(2,1)}, bf16[136,768]{1,0:T(8,128)(2,1)S(1)}, u32[]{:S(2)}) copy-start(bf16[136,768]{1,0:T(8,128)(2,1)S(1)} %collective-permute-done.9.refs_1_.refs_4_) | copy-start | bytes 626692
  32.3 36.9 %collective-permute-start.12 = (bf16[384,768]{1,0:T(8,128)(2,1)}, bf16[384,768]{1,0:T(8,128)(2,1)}, u32[]{:S(2)}, u32[]{:S(2)}) collective-permute-start(bf16[384,768]{1,0:T(8,128)(2,1)} %wol_ref.1), channel_id=1, source_target_pairs={{0,1},{1,0},{2,3},{3,2},{4,5},{5,4},{6,7},{7,6},{8,9},{9,8},{10,11... | collective-permute-start | bytes 1769480 | tf_op jit(solution)/shard_map/ppermute | solution.py:413
  34.7 9.0 %copy-start.2 = (bf16[768,384]{1,0:T(8,128)(2,1)}, bf16[768,384]{1,0:T(8,128)(2,1)S(1)}, u32[]{:S(2)}) copy-start(bf16[768,384]{1,0:T(8,128)(2,1)S(1)} %collective-permute-done.6.refs_2_.refs_3_) | copy-start | bytes 1769476
  34.7 6.7 %collective-permute-start.4 = (bf16[136,768]{1,0:T(8,128)(2,1)S(1)}, bf16[136,768]{1,0:T(8,128)(2,1)S(1)}, u32[]{:S(2)}, u32[]{:S(2)}) collective-permute-start(bf16[136,768]{1,0:T(8,128)(2,1)S(1)} %collective-permute-done.3.refs_0_.refs_3_), channel_id=1, source_target_pairs={{0,4},{4,8},{8,12},{12,14},{14,10},{10,6},{6,2},{2,0},{1,5},{5,9},... | collective-permute-start | bytes 626696 | tf_op jit(solution)/shard_map/ppermute | solution.py:452
  36.9 6.8 %copy-start.3 = (bf16[768,384]{1,0:T(8,128)(2,1)}, bf16[768,384]{1,0:T(8,128)(2,1)S(1)}, u32[]{:S(2)}) copy-start(bf16[768,384]{1,0:T(8,128)(2,1)S(1)} %collective-permute-done.7.refs_4_.refs_5_) | copy-start | bytes 1769476
  36.9 32.2 %collective-permute-start.11 = (f32[16,32,128]{2,1,0:T(8,128)S(1)}, f32[16,32,128]{2,1,0:T(8,128)S(1)}, u32[]{:S(2)}, u32[]{:S(2)}) collective-permute-start(f32[16,32,128]{2,1,0:T(8,128)S(1)} %copy-done.4), channel_id=1, source_target_pairs={{0,1},{1,0},{2,3},{3,2},{4,5},{5,4},{6,7},{7,6},{8,9},{9,8},{10,11... | collective-permute-start | bytes 786440 | tf_op jit(solution)/shard_map/ppermute | solution.py:413
  37.3 45.1 %collective-permute-start.19 = (f32[4,128,128]{2,1,0:T(8,128)}, f32[4,128,128]{2,1,0:T(8,128)}, u32[]{:S(2)}, u32[]{:S(2)}) collective-permute-start(f32[4,128,128]{2,1,0:T(8,128)} %atom_bias.1), channel_id=1, source_target_pairs={{0,1},{1,0},{2,3},{3,2},{4,5},{5,4},{6,7},{7,6},{8,9},{9,8},{10,11... | collective-permute-start | bytes 786440 | tf_op jit(solution)/shard_map/ppermute | solution.py:413
  39.6 20.1 %collective-permute-start.10 = (bf16[136,768]{1,0:T(8,128)(2,1)S(1)}, bf16[136,768]{1,0:T(8,128)(2,1)S(1)}, u32[]{:S(2)}, u32[]{:S(2)}) collective-permute-start(bf16[136,768]{1,0:T(8,128)(2,1)S(1)} %collective-permute-done.9.refs_1_.refs_4_), channel_id=1, source_target_pairs={{4,0},{8,4},{12,8},{14,12},{10,14},{6,10},{2,6},{0,2},{5,1},{9,5},... | collective-permute-start | bytes 626696 | tf_op jit(solution)/shard_map/ppermute | solution.py:455
  41.4 10.4 %copy-start.11 = (bf16[136,768]{1,0:T(8,128)(2,1)}, bf16[136,768]{1,0:T(8,128)(2,1)S(1)}, u32[]{:S(2)}) copy-start(bf16[136,768]{1,0:T(8,128)(2,1)S(1)} %collective-permute-done.4.refs_0_.refs_5_) | copy-start | bytes 626692
  41.4 23.4 %collective-permute-start.5 = (bf16[136,768]{1,0:T(8,128)(2,1)S(1)}, bf16[136,768]{1,0:T(8,128)(2,1)S(1)}, u32[]{:S(2)}, u32[]{:S(2)}) collective-permute-start(bf16[136,768]{1,0:T(8,128)(2,1)S(1)} %collective-permute-done.4.refs_0_.refs_5_), channel_id=1, source_target_pairs={{0,4},{4,8},{8,12},{12,14},{14,10},{10,6},{6,2},{2,0},{1,5},{5,9},... | collective-permute-start | bytes 626696 | tf_op jit(solution)/shard_map/ppermute | solution.py:452
  59.7 0.7 copy-start.12
  64.8 0.7 copy-start.6
  69.1 0.7 copy-start.13
  69.8 12.6 %copy-start.5 = (f32[4,128,128]{2,1,0:T(8,128)S(1)}, f32[4,128,128]{2,1,0:T(8,128)}, u32[]{:S(2)}) copy-start(f32[4,128,128]{2,1,0:T(8,128)} %atom_bias.1) | copy-start | bytes 786436
  77.4 25.0 %copy-start.14 = (bf16[4,32,768]{2,1,0:T(8,128)(2,1)S(1)}, bf16[4,32,768]{2,1,0:T(8,128)(2,1)}, u32[]{:S(2)}) copy-start(bf16[4,32,768]{2,1,0:T(8,128)(2,1)} %get-tuple-element.34) | copy-start | bytes 589828
  77.4 6.9 %collective-permute-start.14 = (bf16[4,32,128]{2,1,0:T(8,128)(2,1)}, bf16[4,32,128]{2,1,0:T(8,128)(2,1)S(1)}, u32[]{:S(2)}, u32[]{:S(2)}) collective-permute-start(bf16[4,32,128]{2,1,0:T(8,128)(2,1)} %get-tuple-element.35.own_ref), channel_id=1, source_target_pairs={{0,2},{2,4},{4,6},{6,8},{8,10},{10,12},{12,14},{1,3},{3,5},{5,7},{... | collective-permute-start | bytes 98312 | tf_op jit(solution)/shard_map/ppermute | solution.py:518
  79.4 6.0 %collective-permute-start.15 = (bf16[4,32,128]{2,1,0:T(8,128)(2,1)}, bf16[4,32,128]{2,1,0:T(8,128)(2,1)S(1)}, u32[]{:S(2)}, u32[]{:S(2)}) collective-permute-start(bf16[4,32,128]{2,1,0:T(8,128)(2,1)} %get-tuple-element.35.own_ref), channel_id=1, source_target_pairs={{2,0},{4,2},{6,4},{8,6},{10,8},{12,10},{14,12},{3,1},{5,3},{7,5},{... | collective-permute-start | bytes 98312 | tf_op jit(solution)/shard_map/ppermute | solution.py:519
  80.9 21.6 %collective-permute-start.13 = (bf16[4,32,768]{2,1,0:T(8,128)(2,1)}, bf16[4,32,768]{2,1,0:T(8,128)(2,1)S(1)}, u32[]{:S(2)}, u32[]{:S(2)}) collective-permute-start(bf16[4,32,768]{2,1,0:T(8,128)(2,1)} %get-tuple-element.34), channel_id=1, source_target_pairs={{0,1},{1,0},{2,3},{3,2},{4,5},{5,4},{6,7},{7,6},{8,9},{9,8},{10,11... | collective-permute-start | bytes 589832 | tf_op jit(solution)/shard_map/ppermute | solution.py:413
  84.3 1.1 %copy-start.16 = (bf16[4,32,128]{2,1,0:T(8,128)(2,1)}, bf16[4,32,128]{2,1,0:T(8,128)(2,1)S(1)}, u32[]{:S(2)}) copy-start(bf16[4,32,128]{2,1,0:T(8,128)(2,1)S(1)} %collective-permute-done.14.left_ref) | copy-start | bytes 98308
  85.4 0.6 copy-start.17
  97.7 3.4 %collective-permute-start.20 = (f32[4,3,128]{2,1,0:T(4,128)}, f32[4,3,128]{2,1,0:T(4,128)S(1)}, u32[]{:S(2)}, u32[]{:S(2)}) collective-permute-start(f32[4,3,128]{2,1,0:T(4,128)} %get-tuple-element.39), channel_id=1, source_target_pairs={{0,1},{1,0},{2,3},{3,2},{4,5},{5,4},{6,7},{7,6},{8,9},{9,8},{10,11... | collective-permute-start | bytes 18440 | tf_op jit(solution)/shard_map/ppermute | solution.py:413
